TPU v7x, 128 devices: a whole 4x4x4 slice. The times are simulated.
128 devices in a mesh: ctx: 8 (over x_hi, y), tile: 16 (over z, x_lo, core).
Axes of the slice: x: 4 (x_hi: 2, x_lo: 2; x = x_hi * 2 + x_lo), y: 4, z: 4, core: 2. Of those that a mesh axis runs over, the one named last changes fastest.
Arguments:
- syndrome_bits: int32 [8, 2, 64, 512], P(None, None, 'ctx', 'tile'), may hold values from 0 to 1
- region_assign: int32 [32, 256], P('ctx', 'tile'), may hold values from 0 to 127
- state_in: bfloat16 [64, 512, 512], P('ctx', 'tile'), may hold values from -3 to 3
- bit_to_candidate: float32 [2, 512], replicated, may hold values from -5 to 5
- bit_to_gate: float32 [2, 512], replicated, may hold values from -5 to 5
- conv_weight: bfloat16 [9, 512, 512], replicated, may hold values from -0.09375 to 0.09375
- gate_weight: bfloat16 [512, 512], replicated, may hold values from -0.25 to 0.25
- gate_bias: float32 [512], replicated, may hold values from -4 to 1
- pool_weight: bfloat16 [512, 1024], replicated, may hold values from -0.25 to 0.25
- region_embed: bfloat16 [1024, 1024], P('ctx'), may hold values from -6 to 6
- attn_norm_gain: float32 [1024], replicated, may hold values from 0.1 to 1.9
- query_weight: bfloat16 [1024, 1024], replicated
- key_weight: bfloat16 [1024, 1024], replicated
- value_weight: bfloat16 [1024, 1024], replicated, may hold values from -0.1875 to 0.1875
- out_weight: bfloat16 [1024, 1024], replicated, may hold values from -0.1875 to 0.1875
- mlp_norm_gain: float32 [1024], replicated, may hold values from 0.1 to 1.9
- mlp_up: bfloat16 [1024, 2048], replicated, may hold values from -0.1875 to 0.1875
- mlp_down: bfloat16 [2048, 1024], replicated, may hold values from -0.125 to 0.125
- return_weight: bfloat16 [1024, 512], replicated, may hold values from -0.1875 to 0.1875
Outputs:
- state_out: bfloat16 [64, 512, 512], P('ctx', 'tile')
- context_out: bfloat16 [1024, 1024], P('ctx')
All inputs are finite; a program needn't handle non-finite values.
Results may differ from a plain program's by a relative error of at most 0.02.
Values may be sent and summed in bfloat16 or wider, within the bound.
A program may use at most 128 MiB of HBM per device.

v0:
```python
import math

import jax
import jax.numpy as jnp
from jax import lax
from jax.sharding import PartitionSpec as P

HEADS = 8
HDIM = 128
ROUNDS = 8


def extended(value, sides, width):
    for axis, dim in sides:
        size, length = (lax.axis_size(axis), value.shape[dim])
        up = [(i, (i + 1) % size) for i in range(size - 1)]
        down = [(j, i) for i, j in up]
        last = lax.slice_in_dim(value, length - width, length, axis=dim)
        first = lax.slice_in_dim(value, 0, width, axis=dim)
        before = lax.ppermute(last, axis, up)
        after = lax.ppermute(first, axis, down)
        value = jnp.concatenate([before, value, after], axis=dim)
    return value


def rms_norm(values, gain):
    return values * lax.rsqrt(jnp.mean(values * values, axis=-1, keepdims=True) + 1e-05) * gain


def advance(
    state, padded, syndrome_now, conv_flat, gate_weight, gate_bias, bit_to_candidate, bit_to_gate
):
    patch_rows, patch_cols, channels = state.shape
    rounded = padded[1 : patch_rows + 1, 1 : patch_cols + 1]
    columns = jnp.concatenate(
        [
            padded[offset_row : offset_row + patch_rows, offset_col : offset_col + patch_cols]
            for offset_row in range(3)
            for offset_col in range(3)
        ],
        axis=-1,
    )
    syndrome_flags = syndrome_now.astype(jnp.float32)
    drive_cand = (
        syndrome_flags[0][..., None] * bit_to_candidate[0]
        + syndrome_flags[1][..., None] * bit_to_candidate[1]
    )
    drive_gate = (
        syndrome_flags[0][..., None] * bit_to_gate[0]
        + syndrome_flags[1][..., None] * bit_to_gate[1]
    )
    candidate = (
        jnp.dot(
            columns.reshape(patch_rows * patch_cols, 9 * channels),
            conv_flat,
            preferred_element_type=jnp.float32,
        ).reshape(patch_rows, patch_cols, channels)
        + drive_cand
    )
    update_gate = jax.nn.sigmoid(
        jnp.dot(
            rounded.reshape(patch_rows * patch_cols, channels),
            gate_weight,
            preferred_element_type=jnp.float32,
        ).reshape(patch_rows, patch_cols, channels)
        + drive_gate
        + gate_bias
    )
    return state + update_gate * (jnp.tanh(candidate) - state)


def region_layer(
    tokens,
    attn_norm_gain,
    query_weight,
    key_weight,
    value_weight,
    out_weight,
    mlp_norm_gain,
    mlp_up,
    mlp_down,
    gather_keys,
):
    token_count = tokens.shape[0]
    normed = rms_norm(tokens, attn_norm_gain).astype(jnp.bfloat16)
    queries = jnp.dot(normed, query_weight, preferred_element_type=jnp.float32).astype(jnp.bfloat16)
    query_heads = queries.reshape(token_count, HEADS, HDIM).transpose(1, 0, 2)
    key_rows = jnp.dot(normed, key_weight, preferred_element_type=jnp.float32).astype(jnp.bfloat16)
    value_rows = jnp.dot(normed, value_weight, preferred_element_type=jnp.float32).astype(
        jnp.bfloat16
    )
    scale = 1.0 / math.sqrt(HDIM)

    def absorb(running, gathered, first_row):
        running_max, denominator, weighted = running
        key_part, value_part = gathered
        part_rows = key_part.shape[0]
        scores = (
            jnp.einsum(
                "hqd,khd->hqk",
                query_heads,
                key_part.reshape(part_rows, HEADS, HDIM),
                preferred_element_type=jnp.float32,
            )
            * scale
        )
        new_max = jnp.maximum(running_max, jnp.max(scores, axis=-1))
        weights = jnp.exp(scores - new_max[..., None])
        denominator = jnp.sum(weights, axis=-1)
        weighted = jnp.einsum(
            "hqk,khd->hqd",
            weights.astype(jnp.bfloat16),
            value_part.reshape(part_rows, HEADS, HDIM),
            preferred_element_type=jnp.float32,
        )
        return (new_max, denominator, weighted)

    start_state = (
        jnp.full((HEADS, token_count), -1e30, jnp.float32),
        jnp.zeros((HEADS, token_count), jnp.float32),
        jnp.zeros((HEADS, token_count, HDIM), jnp.float32),
    )
    running_max, denominator, weighted = gather_keys(key_rows, value_rows, absorb, start_state)
    attention = (
        (weighted / denominator[..., None])
        .transpose(1, 0, 2)
        .reshape(token_count, HEADS * HDIM)
        .astype(jnp.bfloat16)
    )
    attended = tokens + jnp.dot(attention, out_weight, preferred_element_type=jnp.float32)
    hidden = jax.nn.gelu(
        jnp.dot(
            rms_norm(attended, mlp_norm_gain).astype(jnp.bfloat16),
            mlp_up,
            preferred_element_type=jnp.float32,
        )
    ).astype(jnp.bfloat16)
    return (attended + jnp.dot(hidden, mlp_down, preferred_element_type=jnp.float32)).astype(
        jnp.bfloat16
    )


def local(
    syndrome_bits,
    region_assign,
    state_in,
    bit_to_candidate,
    bit_to_gate,
    conv_weight,
    gate_weight,
    gate_bias,
    pool_weight,
    region_embed,
    attn_norm_gain,
    query_weight,
    key_weight,
    value_weight,
    out_weight,
    mlp_norm_gain,
    mlp_up,
    mlp_down,
    return_weight,
):
    state = state_in.astype(jnp.float32)
    patch_rows, patch_cols, channels = state.shape
    conv_flat = conv_weight.reshape(9 * channels, channels)
    layer_weights = (
        attn_norm_gain,
        query_weight,
        key_weight,
        value_weight,
        out_weight,
        mlp_norm_gain,
        mlp_up,
        mlp_down,
    )
    context_out = None
    for round_index in range(ROUNDS):
        if round_index == ROUNDS // 2:
            pooled = (
                state.reshape(patch_rows // 2, 2, patch_cols // 2, 2, channels)
                .mean(axis=(1, 3))
                .astype(jnp.bfloat16)
            )
            band_tokens = region_embed.shape[0]
            member = (
                region_assign.reshape(1, -1) == jnp.arange(band_tokens, dtype=jnp.int32)[:, None]
            ).astype(jnp.float32)
            projected = jnp.dot(
                pooled.reshape(-1, channels), pool_weight, preferred_element_type=jnp.float32
            )
            partial_value = jnp.dot(member, projected, precision=lax.Precision.HIGHEST)
            share_rows = band_tokens // lax.axis_size("tile")
            first_row = lax.axis_index("tile") * share_rows
            summed = lax.psum_scatter(
                partial_value.astype(jnp.bfloat16), "tile", scatter_dimension=0, tiled=True
            ).astype(jnp.float32)
            embed_rows = lax.dynamic_slice_in_dim(region_embed, first_row, share_rows, 0).astype(
                jnp.float32
            )
            tokens = summed + embed_rows

            def gather_split(key_rows, value_rows, absorb, start_state):
                return absorb(
                    start_state,
                    (
                        lax.all_gather(key_rows, ("ctx", "tile"), axis=0, tiled=True),
                        lax.all_gather(value_rows, ("ctx", "tile"), axis=0, tiled=True),
                    ),
                    jnp.int32(0),
                )

            local_context = region_layer(tokens, *layer_weights, gather_split)
            context_out = lax.all_gather(local_context, "tile", axis=0, tiled=True)
            returned = jnp.dot(context_out, return_weight, preferred_element_type=jnp.float32)
            share_back = jnp.dot(member.T, returned, precision=lax.Precision.HIGHEST).reshape(
                patch_rows // 2, patch_cols // 2, channels
            )
            state = (
                state.reshape(patch_rows // 2, 2, patch_cols // 2, 2, channels)
                + share_back[:, None, :, None, :]
            ).reshape(patch_rows, patch_cols, channels)
        rounded = state.astype(jnp.bfloat16)
        padded = extended(rounded, (("ctx", 0), ("tile", 1)), 1)
        state = advance(
            state,
            padded,
            syndrome_bits[round_index],
            conv_flat,
            gate_weight,
            gate_bias,
            bit_to_candidate,
            bit_to_gate,
        )
    return (state.astype(jnp.bfloat16), context_out)


def solution(mesh):
    return jax.shard_map(
        local,
        mesh=mesh,
        in_specs=(
            P(None, None, "ctx", "tile"),
            P("ctx", "tile"),
            P("ctx", "tile", None),
            P(),
            P(),
            P(),
            P(),
            P(),
            P(),
            P("ctx", None),
            P(),
            P(),
            P(),
            P(),
            P(),
            P(),
            P(),
            P(),
            P(),
        ),
        out_specs=(P("ctx", "tile", None), P("ctx", None)),
        check_vma=False,
    )
```

profile of v0, /device:TPU:6, one launch (start us, length us, event | category | flops | bytes accessed | tf_op | source)
XLA Modules:
  0.0 688.0 jit_solution(17125236643354716497)
XLA Ops:
  8.2 5.8 collective-permute-start.1
  13.9 1.9 collective-permute-start
  17.5 5.9 collective-permute-done
  24.4 1.9 collective-permute-start.2
  27.1 3.6 collective-permute-start.3
  35.1 1.9 collective-permute-start.4
  37.0 7.5 %collective-permute-start.5 = (bf16[1,32,512]{2,1,0:T(8,128)(2,1)S(1)}, bf16[1,32,512]{2,1,0:T(8,128)(2,1)S(1)}, u32[]{:S(2)}, u32[]{:S(2)}) collective-permute-start(bf16[1,32,512]{2,1,0:T(8,128)(2,1)S(1)} %get-tuple-element.47), channel_id=1, source_target_pairs={{16,0},{32,16},{48,32},{64,48},{80,64},{96,80},{112,96},{17,1},{33... | collective-permute-start | bytes 98312 | tf_op jit(solution)/shard_map/ppermute | solution.py:21
  44.6 1.6 collective-permute-done.5
  46.2 2.0 collective-permute-start.7
  48.3 2.5 collective-permute-start.6
  50.8 2.6 collective-permute-done.6
  53.9 1.4 fusion.75
  55.8 1.9 collective-permute-start.8
  57.7 8.1 %collective-permute-start.9 = (bf16[1,32,512]{2,1,0:T(8,128)(2,1)S(1)}, bf16[1,32,512]{2,1,0:T(8,128)(2,1)S(1)}, u32[]{:S(2)}, u32[]{:S(2)}) collective-permute-start(bf16[1,32,512]{2,1,0:T(8,128)(2,1)S(1)} %get-tuple-element.45), channel_id=1, source_target_pairs={{16,0},{32,16},{48,32},{64,48},{80,64},{96,80},{112,96},{17,1},{33... | collective-permute-start | bytes 98312 | tf_op jit(solution)/shard_map/ppermute | solution.py:21
  65.9 1.6 collective-permute-done.9
  67.5 1.9 collective-permute-start.11
  69.4 2.4 collective-permute-start.10
  71.8 2.7 collective-permute-done.10
  75.1 1.4 fusion.73
  77.7 1.9 collective-permute-start.12
  79.7 7.8 %collective-permute-start.13 = (bf16[1,32,512]{2,1,0:T(8,128)(2,1)S(1)}, bf16[1,32,512]{2,1,0:T(8,128)(2,1)S(1)}, u32[]{:S(2)}, u32[]{:S(2)}) collective-permute-start(bf16[1,32,512]{2,1,0:T(8,128)(2,1)S(1)} %get-tuple-element.43), channel_id=1, source_target_pairs={{16,0},{32,16},{48,32},{64,48},{80,64},{96,80},{112,96},{17,1},{33... | collective-permute-start | bytes 98312 | tf_op jit(solution)/shard_map/ppermute | solution.py:21
  87.5 1.6 collective-permute-done.13
  89.1 1.9 collective-permute-start.15
  91.0 2.9 collective-permute-start.14
  94.0 2.1 collective-permute-done.14
  97.3 3.8 fusion.71
  102.3 1.5 fusion.187
  105.0 63.2 %reduce-scatter.2.cloned.1.call-done = bf16[8,1024]{1,0:T(8,128)(2,1)} async-done(((bf16[128,1024]{1,0:T(8,128)(2,1)}), bf16[8,1024]{1,0:T(8,128)(2,1)}) %reduce-scatter.2.cloned.1.call-update) | async-done | bytes 16400 | tf_op jit(solution)/shard_map/reduce_scatter | solution.py:195
  169.9 2.6 convolution_convert_fusion.2
  172.7 2.6 convolution_convert_fusion.1
  175.4 194.0 %all-gather.3.cloned.1.call-done = bf16[1024,1024]{1,0:T(8,128)(2,1)} async-done(((bf16[8,1024]{1,0:T(8,128)(2,1)}), bf16[1024,1024]{1,0:T(8,128)(2,1)}) %all-gather.3.cloned.1.call-update) | async-done | bytes 2097168 | tf_op jit(solution)/shard_map/all_gather | solution.py:207
  369.4 2.6 fusion.179
  372.2 193.8 %all-gather.5.cloned.1.call-done = bf16[1024,1024]{1,0:T(8,128)(2,1)} async-done(((bf16[8,1024]{1,0:T(8,128)(2,1)}), bf16[1024,1024]{1,0:T(8,128)(2,1)}) %all-gather.5.cloned.1.call-update) | async-done | bytes 2097168 | tf_op jit(solution)/shard_map/all_gather | solution.py:208
  566.0 3.2 multiply_reduce_fusion
  569.2 4.8 fusion.88
  573.9 18.0 %all_gather.11 = bf16[128,1024]{1,0:T(8,128)(2,1)S(1)} all-gather(bf16[8,1024]{1,0:T(8,128)(2,1)S(1)} %fusion.88), channel_id=1, replica_groups=mesh['ctx'=8,'tile'=16] {'tile'}, dimensions={0}, use_global_device_ids=true | all-gather | bytes 278528 | tf_op jit(solution)/shard_map/all_gather | solution.py:214
  593.1 2.8 collective-permute-start.16
  596.0 6.6 collective-permute-start.17
  602.6 1.6 collective-permute-done.17
  604.2 3.0 collective-permute-start.19
  607.2 1.9 collective-permute-start.18
  609.1 3.2 collective-permute-done.18
  612.9 3.9 fusion.69
  617.2 1.9 collective-permute-start.20
  619.1 8.1 %collective-permute-start.21 = (bf16[1,32,512]{2,1,0:T(8,128)(2,1)S(1)}, bf16[1,32,512]{2,1,0:T(8,128)(2,1)S(1)}, u32[]{:S(2)}, u32[]{:S(2)}) collective-permute-start(bf16[1,32,512]{2,1,0:T(8,128)(2,1)S(1)} %get-tuple-element.39), channel_id=1, source_target_pairs={{16,0},{32,16},{48,32},{64,48},{80,64},{96,80},{112,96},{17,1},{33... | collective-permute-start | bytes 98312 | tf_op jit(solution)/shard_map/ppermute | solution.py:21
  627.3 1.6 collective-permute-done.21
  628.9 1.9 collective-permute-start.23
  630.8 2.4 collective-permute-start.22
  633.3 2.7 collective-permute-done.22
  636.5 1.4 fusion.67
  638.4 1.9 collective-permute-start.24
  640.3 7.8 %collective-permute-start.25 = (bf16[1,32,512]{2,1,0:T(8,128)(2,1)S(1)}, bf16[1,32,512]{2,1,0:T(8,128)(2,1)S(1)}, u32[]{:S(2)}, u32[]{:S(2)}) collective-permute-start(bf16[1,32,512]{2,1,0:T(8,128)(2,1)S(1)} %get-tuple-element.37), channel_id=1, source_target_pairs={{16,0},{32,16},{48,32},{64,48},{80,64},{96,80},{112,96},{17,1},{33... | collective-permute-start | bytes 98312 | tf_op jit(solution)/shard_map/ppermute | solution.py:21
  648.2 1.6 collective-permute-done.25
  649.8 1.9 collective-permute-start.27
  651.7 2.4 collective-permute-start.26
  654.1 2.7 collective-permute-done.26
  657.3 1.4 fusion.65
  659.2 1.9 collective-permute-start.28
  661.1 7.8 %collective-permute-start.29 = (bf16[1,32,512]{2,1,0:T(8,128)(2,1)S(1)}, bf16[1,32,512]{2,1,0:T(8,128)(2,1)S(1)}, u32[]{:S(2)}, u32[]{:S(2)}) collective-permute-start(bf16[1,32,512]{2,1,0:T(8,128)(2,1)S(1)} %get-tuple-element.35), channel_id=1, source_target_pairs={{16,0},{32,16},{48,32},{64,48},{80,64},{96,80},{112,96},{17,1},{33... | collective-permute-start | bytes 98312 | tf_op jit(solution)/shard_map/ppermute | solution.py:21
  669.0 1.6 collective-permute-done.29
  670.6 1.9 collective-permute-start.31
  672.5 2.4 collective-permute-start.30
  675.0 2.7 collective-permute-done.30
  678.2 1.4 fusion.63
  (191 shorter events, 23.5 us)
Async XLA Ops:
  7.2 362.2 %copy-start = (bf16[1024,1024]{1,0:T(8,128)(2,1)S(1)}, bf16[1024,1024]{1,0:T(8,128)(2,1)}, u32[]{:S(2)}) copy-start(bf16[1024,1024]{1,0:T(8,128)(2,1)} %param.30) | copy-start | bytes 6291460
  7.2 25.2 %copy-start.2 = (bf16[8,32,512]{2,1,0:T(8,128)(2,1)S(1)}, bf16[8,32,512]{2,1,0:T(8,128)(2,1)}, u32[]{:S(2)}) copy-start(bf16[8,32,512]{2,1,0:T(8,128)(2,1)} %param.21) | copy-start | bytes 786436
  7.2 161.0 %reduce-scatter.2.cloned.1.call-start = ((), (), s32[]{:S(2)}) async-start(), calls=%async_computation.1 | async-start | bytes 278528 | tf_op jit(solution)/shard_map/reduce_scatter | solution.py:195
  8.2 16.2 %collective-permute-start.1 = (bf16[1,32,512]{2,1,0:T(8,128)(2,1)S(1)}, bf16[1,32,512]{2,1,0:T(8,128)(2,1)S(1)}, u32[]{:S(2)}, u32[]{:S(2)}) collective-permute-start(bf16[1,32,512]{2,1,0:T(8,128)(2,1)S(1)} %get-tuple-element.48), channel_id=1, source_target_pairs={{16,0},{32,16},{48,32},{64,48},{80,64},{96,80},{112,96},{17,1},{33... | collective-permute-start | bytes 98312 | tf_op jit(solution)/shard_map/ppermute | solution.py:21
  13.9 9.4 %collective-permute-start = (bf16[1,32,512]{2,1,0:T(8,128)(2,1)S(1)}, bf16[1,32,512]{2,1,0:T(8,128)(2,1)S(1)}, u32[]{:S(2)}, u32[]{:S(2)}) collective-permute-start(bf16[1,32,512]{2,1,0:T(8,128)(2,1)S(1)} %get-tuple-element.49), channel_id=1, source_target_pairs={{0,16},{16,32},{32,48},{48,64},{64,80},{80,96},{96,112},{1,17},{17... | collective-permute-start | bytes 98312 | tf_op jit(solution)/shard_map/ppermute | solution.py:20
  24.4 6.3 collective-permute-start.2
  27.1 5.1 collective-permute-start.3
  30.8 2.4 copy-start.8
  33.2 1.4 copy-start.9
  33.2 1.4 copy-start.12
  35.1 9.5 %collective-permute-start.4 = (bf16[1,32,512]{2,1,0:T(8,128)(2,1)S(1)}, bf16[1,32,512]{2,1,0:T(8,128)(2,1)S(1)}, u32[]{:S(2)}, u32[]{:S(2)}) collective-permute-start(bf16[1,32,512]{2,1,0:T(8,128)(2,1)S(1)} %get-tuple-element.46), channel_id=1, source_target_pairs={{0,16},{16,32},{32,48},{48,64},{64,80},{80,96},{96,112},{1,17},{17... | collective-permute-start | bytes 98312 | tf_op jit(solution)/shard_map/ppermute | solution.py:20
  37.0 9.1 %collective-permute-start.5 = (bf16[1,32,512]{2,1,0:T(8,128)(2,1)S(1)}, bf16[1,32,512]{2,1,0:T(8,128)(2,1)S(1)}, u32[]{:S(2)}, u32[]{:S(2)}) collective-permute-start(bf16[1,32,512]{2,1,0:T(8,128)(2,1)S(1)} %get-tuple-element.47), channel_id=1, source_target_pairs={{16,0},{32,16},{48,32},{64,48},{80,64},{96,80},{112,96},{17,1},{33... | collective-permute-start | bytes 98312 | tf_op jit(solution)/shard_map/ppermute | solution.py:21
  46.2 4.6 collective-permute-start.7
  48.3 5.1 collective-permute-start.6
  55.8 10.1 %collective-permute-start.8 = (bf16[1,32,512]{2,1,0:T(8,128)(2,1)S(1)}, bf16[1,32,512]{2,1,0:T(8,128)(2,1)S(1)}, u32[]{:S(2)}, u32[]{:S(2)}) collective-permute-start(bf16[1,32,512]{2,1,0:T(8,128)(2,1)S(1)} %get-tuple-element.44), channel_id=1, source_target_pairs={{0,16},{16,32},{32,48},{48,64},{64,80},{80,96},{96,112},{1,17},{17... | collective-permute-start | bytes 98312 | tf_op jit(solution)/shard_map/ppermute | solution.py:20
  57.7 9.7 %collective-permute-start.9 = (bf16[1,32,512]{2,1,0:T(8,128)(2,1)S(1)}, bf16[1,32,512]{2,1,0:T(8,128)(2,1)S(1)}, u32[]{:S(2)}, u32[]{:S(2)}) collective-permute-start(bf16[1,32,512]{2,1,0:T(8,128)(2,1)S(1)} %get-tuple-element.45), channel_id=1, source_target_pairs={{16,0},{32,16},{48,32},{64,48},{80,64},{96,80},{112,96},{17,1},{33... | collective-permute-start | bytes 98312 | tf_op jit(solution)/shard_map/ppermute | solution.py:21
  67.5 4.4 collective-permute-start.11
  69.4 5.1 collective-permute-start.10
  76.5 17.4 %copy-start.7 = (s32[4,16]{1,0:T(4,128)S(1)}, s32[4,16]{1,0:T(4,128)}, u32[]{:S(2)}) copy-start(s32[4,16]{1,0:T(4,128)} %param.20) | copy-start | bytes 772
  77.7 9.8 %collective-permute-start.12 = (bf16[1,32,512]{2,1,0:T(8,128)(2,1)S(1)}, bf16[1,32,512]{2,1,0:T(8,128)(2,1)S(1)}, u32[]{:S(2)}, u32[]{:S(2)}) collective-permute-start(bf16[1,32,512]{2,1,0:T(8,128)(2,1)S(1)} %get-tuple-element.42), channel_id=1, source_target_pairs={{0,16},{16,32},{32,48},{48,64},{64,80},{80,96},{96,112},{1,17},{17... | collective-permute-start | bytes 98312 | tf_op jit(solution)/shard_map/ppermute | solution.py:20
  79.7 9.4 %collective-permute-start.13 = (bf16[1,32,512]{2,1,0:T(8,128)(2,1)S(1)}, bf16[1,32,512]{2,1,0:T(8,128)(2,1)S(1)}, u32[]{:S(2)}, u32[]{:S(2)}) collective-permute-start(bf16[1,32,512]{2,1,0:T(8,128)(2,1)S(1)} %get-tuple-element.43), channel_id=1, source_target_pairs={{16,0},{32,16},{48,32},{64,48},{80,64},{96,80},{112,96},{17,1},{33... | collective-permute-start | bytes 98312 | tf_op jit(solution)/shard_map/ppermute | solution.py:21
  89.1 4.9 collective-permute-start.15
  91.0 5.1 collective-permute-start.14
  96.3 1.0 copy-start.13
  97.3 3.8 copy-start.10
  101.6 67.5 %copy-start.6 = (f32[1024]{0:T(1024)S(1)}, f32[1024]{0:T(1024)}, u32[]{:S(2)}) copy-start(f32[1024]{0:T(1024)} %param.29) | copy-start | bytes 12292
  104.9 264.4 %all-gather.3.cloned.1.call-start = ((), (), s32[]{:S(2)}) async-start(), calls=%async_computation.2 | async-start | bytes 2113536 | tf_op jit(solution)/shard_map/all_gather | solution.py:207
  172.5 393.5 %all-gather.5.cloned.1.call-start = ((), (), s32[]{:S(2)}) async-start(), calls=%async_computation.3 | async-start | bytes 2113536 | tf_op jit(solution)/shard_map/all_gather | solution.py:208
  175.3 390.6 %copy-start.4 = (bf16[8,1024]{1,0:T(8,128)(2,1)S(1)}, bf16[8,1024]{1,0:T(8,128)(2,1)}, u32[]{:S(2)}) copy-start(bf16[8,1024]{1,0:T(8,128)(2,1)} %reduce-scatter.2.cloned.1.call-done) | copy-start | bytes 49156
  372.0 197.2 %copy-start.5 = (f32[1024]{0:T(1024)S(1)}, f32[1024]{0:T(1024)}, u32[]{:S(2)}) copy-start(f32[1024]{0:T(1024)} %param.34) | copy-start | bytes 12292
  569.2 22.7 %copy-start.3 = (bf16[1024,512]{1,0:T(8,128)(2,1)S(1)}, bf16[1024,512]{1,0:T(8,128)(2,1)}, u32[]{:S(2)}) copy-start(bf16[1024,512]{1,0:T(8,128)(2,1)} %param.37) | copy-start | bytes 3145732
  593.1 9.5 %collective-permute-start.16 = (bf16[1,32,512]{2,1,0:T(8,128)(2,1)S(1)}, bf16[1,32,512]{2,1,0:T(8,128)(2,1)S(1)}, u32[]{:S(2)}, u32[]{:S(2)}) collective-permute-start(bf16[1,32,512]{2,1,0:T(8,128)(2,1)S(1)} %get-tuple-element.40), channel_id=1, source_target_pairs={{0,16},{16,32},{32,48},{48,64},{64,80},{80,96},{96,112},{1,17},{17... | collective-permute-start | bytes 98312 | tf_op jit(solution)/shard_map/ppermute | solution.py:20
  596.0 8.2 %collective-permute-start.17 = (bf16[1,32,512]{2,1,0:T(8,128)(2,1)S(1)}, bf16[1,32,512]{2,1,0:T(8,128)(2,1)S(1)}, u32[]{:S(2)}, u32[]{:S(2)}) collective-permute-start(bf16[1,32,512]{2,1,0:T(8,128)(2,1)S(1)} %get-tuple-element.41), channel_id=1, source_target_pairs={{16,0},{32,16},{48,32},{64,48},{80,64},{96,80},{112,96},{17,1},{33... | collective-permute-start | bytes 98312 | tf_op jit(solution)/shard_map/ppermute | solution.py:21
  604.2 4.9 collective-permute-start.19
  607.2 5.1 collective-permute-start.18
  612.8 3.9 copy-start.11
  612.8 23.7 %slice-start = ((s8[4718592]{0:T(1024)(128)(4,1)}), s8[4194304]{0:T(1024)(128)(4,1)S(1)}, s32[]{:S(2)}) async-start(s8[4718592]{0:T(1024)(128)(4,1)} %bitcast.207), calls=%async_computation.4 | async-start | bytes 8388608
  616.8 19.7 %slice-start.1 = ((s8[4718592]{0:T(1024)(128)(4,1)}), s8[524288]{0:T(1024)(128)(4,1)S(1)}, s32[]{:S(2)}) async-start(s8[4718592]{0:T(1024)(128)(4,1)} %bitcast.207), calls=%async_computation.5 | async-start | bytes 1048576
  617.2 10.1 %collective-permute-start.20 = (bf16[1,32,512]{2,1,0:T(8,128)(2,1)S(1)}, bf16[1,32,512]{2,1,0:T(8,128)(2,1)S(1)}, u32[]{:S(2)}, u32[]{:S(2)}) collective-permute-start(bf16[1,32,512]{2,1,0:T(8,128)(2,1)S(1)} %get-tuple-element.38), channel_id=1, source_target_pairs={{0,16},{16,32},{32,48},{48,64},{64,80},{80,96},{96,112},{1,17},{17... | collective-permute-start | bytes 98312 | tf_op jit(solution)/shard_map/ppermute | solution.py:20
  619.1 9.7 %collective-permute-start.21 = (bf16[1,32,512]{2,1,0:T(8,128)(2,1)S(1)}, bf16[1,32,512]{2,1,0:T(8,128)(2,1)S(1)}, u32[]{:S(2)}, u32[]{:S(2)}) collective-permute-start(bf16[1,32,512]{2,1,0:T(8,128)(2,1)S(1)} %get-tuple-element.39), channel_id=1, source_target_pairs={{16,0},{32,16},{48,32},{64,48},{80,64},{96,80},{112,96},{17,1},{33... | collective-permute-start | bytes 98312 | tf_op jit(solution)/shard_map/ppermute | solution.py:21
  628.9 4.4 collective-permute-start.23
  630.8 5.1 collective-permute-start.22
  638.4 9.8 %collective-permute-start.24 = (bf16[1,32,512]{2,1,0:T(8,128)(2,1)S(1)}, bf16[1,32,512]{2,1,0:T(8,128)(2,1)S(1)}, u32[]{:S(2)}, u32[]{:S(2)}) collective-permute-start(bf16[1,32,512]{2,1,0:T(8,128)(2,1)S(1)} %get-tuple-element.36), channel_id=1, source_target_pairs={{0,16},{16,32},{32,48},{48,64},{64,80},{80,96},{96,112},{1,17},{17... | collective-permute-start | bytes 98312 | tf_op jit(solution)/shard_map/ppermute | solution.py:20
  640.3 9.4 %collective-permute-start.25 = (bf16[1,32,512]{2,1,0:T(8,128)(2,1)S(1)}, bf16[1,32,512]{2,1,0:T(8,128)(2,1)S(1)}, u32[]{:S(2)}, u32[]{:S(2)}) collective-permute-start(bf16[1,32,512]{2,1,0:T(8,128)(2,1)S(1)} %get-tuple-element.37), channel_id=1, source_target_pairs={{16,0},{32,16},{48,32},{64,48},{80,64},{96,80},{112,96},{17,1},{33... | collective-permute-start | bytes 98312 | tf_op jit(solution)/shard_map/ppermute | solution.py:21
  649.8 4.4 collective-permute-start.27
  651.7 5.1 collective-permute-start.26
  659.2 9.8 %collective-permute-start.28 = (bf16[1,32,512]{2,1,0:T(8,128)(2,1)S(1)}, bf16[1,32,512]{2,1,0:T(8,128)(2,1)S(1)}, u32[]{:S(2)}, u32[]{:S(2)}) collective-permute-start(bf16[1,32,512]{2,1,0:T(8,128)(2,1)S(1)} %get-tuple-element.34), channel_id=1, source_target_pairs={{0,16},{16,32},{32,48},{48,64},{64,80},{80,96},{96,112},{1,17},{17... | collective-permute-start | bytes 98312 | tf_op jit(solution)/shard_map/ppermute | solution.py:20
  661.1 9.4 %collective-permute-start.29 = (bf16[1,32,512]{2,1,0:T(8,128)(2,1)S(1)}, bf16[1,32,512]{2,1,0:T(8,128)(2,1)S(1)}, u32[]{:S(2)}, u32[]{:S(2)}) collective-permute-start(bf16[1,32,512]{2,1,0:T(8,128)(2,1)S(1)} %get-tuple-element.35), channel_id=1, source_target_pairs={{16,0},{32,16},{48,32},{64,48},{80,64},{96,80},{112,96},{17,1},{33... | collective-permute-start | bytes 98312 | tf_op jit(solution)/shard_map/ppermute | solution.py:21
  670.6 4.4 collective-permute-start.31
  672.5 5.1 collective-permute-start.30
  678.2 3.3 copy-start.1
Sparse Core Ops, SparseCore 0:
  105.1 63.1 reduce-scatter.1
  172.6 196.6 all-gather.2
  371.7 194.2 all-gather.4
where the time goes:
time: 694 us; the launch traced here: 688 us
  waiting for transfers between devices  487 us (70%)
  starting transfers between devices  113 us (16%)
  matrix products  39.9 us (6%)
  blocking collectives  18 us (3%)
  between operations  15.2 us (2%)
  local copies, waits for them, and re-layouts  8.39 us (1%)
    all_gather x1, waiting for transfers between devices, gather_split(): lax.all_gather(key_rows, ('ctx', 'tile'), axis=0, tiled=True)  194 us
    all_gather x1, waiting for transfers between devices, gather_split(): lax.all_gather(value_rows, ('ctx', 'tile'), axis=0, tiled=True)  194 us
    ppermute x16, starting transfers between devices, extended(): after = lax.ppermute(first, axis, down)  78 us
    reduce_scatter x1, waiting for transfers between devices, local(): lax.psum_scatter(partial_value.astype(jnp.bfloat16), 'tile', scatter_dime...  63.2 us
    ppermute x16, starting transfers between devices, extended(): before = lax.ppermute(last, axis, up)  35 us
    ppermute x16, waiting for transfers between devices, extended(): before = lax.ppermute(last, axis, up)  24.5 us
    all_gather x1, blocking collectives, local(): context_out = lax.all_gather(local_context, 'tile', axis=0, tiled=True)  18 us
    dot_general x8, matrix products, advance(): jnp.dot(columns.reshape(patch_rows * patch_cols, 9 * channels), conv_flat...  16.1 us
  transfers between devices with their start and end apart: 35, of which 19 were waited for; matrix products, arithmetic and copies ran while one was open for 1% of the time, Pallas kernels for 0%

commit v1 on v0

v1 whole, which is shorter than its diff:
```python
import functools
import math

import jax
import jax.numpy as jnp
from jax import lax
from jax.experimental import pallas as pl
from jax.experimental.pallas import tpu as pltpu
from jax.sharding import PartitionSpec as P

MESH = pl.DeviceIdType.MESH
BF16 = jnp.bfloat16
F32 = jnp.float32

HEADS = 8
HDIM = 128
ROUNDS = 8
HALF = 4
C = 512
E = 1024
ROWS = 16
COLS = 48
OWN_ROWS = slice(4, 12)
LANES = 128
ASSIGN = 40

MOVES = ((-1, 0), (1, 0), (0, -1), (0, 1), (-1, -1), (-1, 1), (1, -1), (1, 1))


def dot(left, right):
    return jnp.dot(left, right, preferred_element_type=F32)


def rms_norm(values, gain):
    return values * lax.rsqrt(jnp.mean(values * values, axis=-1, keepdims=True) + 1e-05) * gain


def window(
    extra_in,
    state_in,
    bit_to_candidate,
    bit_to_gate,
    conv_weight,
    gate_weight,
    gate_bias,
    pool_weight,
    region_embed,
    attn_norm_gain,
    query_weight,
    key_weight,
    value_weight,
    out_weight,
    mlp_norm_gain,
    mlp_up,
    mlp_down,
    return_weight,
    state_out,
    context_out,
    state,
    taps,
    extra,
    extra_low,
    drive,
    conv_w,
    gate_w,
    pool_w,
    embed_w,
    qkv_w,
    out_w,
    up_w,
    down_w,
    return_w,
    edge_ns,
    edge_ew,
    extra_ns,
    extra_ew,
    halo_ns,
    halo_ew,
    halo_corner,
    halo_extra_ns,
    halo_extra_ew,
    halo_extra_corner,
    partial_send,
    partial_recv,
    summed_all,
    queries,
    keys_values,
    attention_all,
    attention_full,
    weight_sem,
    edge_sem,
    halo_send,
    halo_recv,
    tile_send,
    tile_recv,
    ctx_send,
    ctx_recv,
):
    g, t = lax.axis_index("ctx"), lax.axis_index("tile")
    ctx_size, tile_size = 8, 16
    head, part = t // 2, lax.rem(t, 2)

    head_cols = pl.ds(pl.multiple_of(head * HDIM, HDIM), HDIM)
    edge_copies = [
        pltpu.make_async_copy(state_in, edge_ns.at[0], edge_sem.at[0]),
        pltpu.make_async_copy(state_in.at[:, 0:8], edge_ew.at[0, 0], edge_sem.at[1]),
        pltpu.make_async_copy(state_in.at[:, 24:32], edge_ew.at[0, 1], edge_sem.at[2]),
        pltpu.make_async_copy(extra_in, extra_ns, edge_sem.at[3]),
        pltpu.make_async_copy(extra_in.at[:, 0:8], extra_ew.at[0], edge_sem.at[4]),
        pltpu.make_async_copy(extra_in.at[:, 24:32], extra_ew.at[1], edge_sem.at[5]),
    ]
    weight_copies = [
        pltpu.make_async_copy(src, dst, weight_sem.at[i])
        for i, (src, dst) in enumerate(
            (
                (conv_weight, conv_w),
                (gate_weight, gate_w),
                (pool_weight, pool_w),
                (region_embed, embed_w),
                (query_weight.at[:, head_cols], qkv_w.at[0]),
                (key_weight.at[:, head_cols], qkv_w.at[1]),
                (value_weight.at[:, head_cols], qkv_w.at[2]),
                (out_weight, out_w),
                (mlp_up, up_w),
                (mlp_down, down_w),
                (return_weight, return_w),
            )
        )
    ]
    for copy in edge_copies:
        copy.start()
    for copy in weight_copies:
        copy.start()

    def inside(move, sign):
        dg, dt = move
        peer_g, peer_t = g + sign * dg, t + sign * dt
        return (peer_g >= 0) & (peer_g < ctx_size) & (peer_t >= 0) & (peer_t < tile_size)

    barrier = pltpu.get_barrier_semaphore()
    heard = jnp.int32(0)
    for move in MOVES[4:]:
        @pl.when(inside(move, 1))
        def _(move=move):
            pl.semaphore_signal(
                barrier, 1, device_id=(g + move[0], t + move[1]), device_id_type=MESH
            )
        heard += inside(move, -1).astype(jnp.int32)
    for step in range(1, ctx_size):
        pl.semaphore_signal(
            barrier, 1, device_id=(lax.rem(g + step, ctx_size), t), device_id_type=MESH
        )
    for step in range(1, tile_size):
        pl.semaphore_signal(
            barrier, 1, device_id=(g, lax.rem(t + step, tile_size)), device_id_type=MESH
        )

    state[...] = jnp.zeros_like(state)
    extra[...] = jnp.zeros_like(extra)

    lane_row = lax.broadcasted_iota(jnp.int32, (LANES, 2 * C), 0)
    both = jnp.concatenate([bit_to_candidate[...], bit_to_gate[...]], axis=1)
    bias = jnp.concatenate([jnp.zeros_like(gate_bias[...]), gate_bias[...]], axis=1)
    both_high = both.astype(BF16).astype(F32)
    both_low = both - both_high
    bias_high = bias.astype(BF16).astype(F32)
    bias_low = bias - bias_high
    even = lax.rem(lane_row, 2) == 0
    drive[...] = jnp.where(
        lane_row < 16,
        jnp.where(even, both_high[0:1], both_high[1:2]),
        jnp.where(
            lane_row < 32,
            jnp.where(even, both_low[0:1], both_low[1:2]),
            jnp.where(
                lane_row == 32, bias_high, jnp.where(lane_row == 33, bias_low, 0.0)
            ),
        ),
    )

    column = lax.broadcasted_iota(jnp.int32, (COLS, 1), 0)
    column_inside = ~(
        ((t == 0) & (column >= 40))
        | ((t == tile_size - 1) & (column >= 32) & (column < 40))
    )

    pl.semaphore_wait(barrier, heard + (ctx_size - 1) + (tile_size - 1))

    def halo_parts(move, half):
        dg, dt = move
        index = MOVES.index(move)
        rows = {0: slice(0, 8), -1: slice(0, 4), 1: slice(4, 8)}[dg]
        side = 0 if dt == -1 else 1
        if dt == 0:
            source, target = edge_ns.at[half, rows], halo_ns.at[half, index]
            more, more_target = extra_ns.at[rows], halo_extra_ns.at[index]
        elif dg == 0:
            source, target = edge_ew.at[half, side], halo_ew.at[half, side]
            more, more_target = extra_ew.at[side], halo_extra_ew.at[side]
        else:
            source, target = edge_ew.at[half, side, rows], halo_corner.at[half, index - 4]
            more, more_target = extra_ew.at[side, rows], halo_extra_corner.at[index - 4]
        return source, target, more, more_target

    def halo_copy(move, half):
        source, target, _, _ = halo_parts(move, half)
        index = MOVES.index(move)
        return pltpu.make_async_remote_copy(
            src_ref=source,
            dst_ref=target,
            send_sem=halo_send.at[half, index],
            recv_sem=halo_recv.at[half, index],
            device_id=(g + move[0], t + move[1]),
            device_id_type=MESH,
        )

    def extra_copy(move):
        _, _, source, target = halo_parts(move, 0)
        index = MOVES.index(move)
        return pltpu.make_async_remote_copy(
            src_ref=source,
            dst_ref=target,
            send_sem=halo_send.at[2, index],
            recv_sem=halo_recv.at[2, index],
            device_id=(g + move[0], t + move[1]),
            device_id_type=MESH,
        )

    def place(move):
        dg, dt = move
        rows = {0: slice(4, 12), -1: slice(12, 16), 1: slice(0, 4)}[dg]
        cols = {0: slice(0, 32), -1: slice(32, 40), 1: slice(40, 48)}[dt]
        return rows, cols

    def exchange(half, first):
        for move in MOVES:
            @pl.when(inside(move, 1))
            def _(move=move):
                halo_copy(move, half).start()
                if first:
                    extra_copy(move).start()
        if first:
            state[OWN_ROWS, 0:32] = edge_ns[0].astype(F32)
            extra[OWN_ROWS, 0:32] = extra_ns[...].astype(F32)
        for move in MOVES:
            @pl.when(inside(move, -1))
            def _(move=move):
                rows, cols = place(move)
                copy = halo_copy(move, half)
                copy.wait_recv()
                _, target, _, more_target = halo_parts(move, half)
                state[rows, cols] = target[...].astype(F32)
                if first:
                    extra_copy(move).wait_recv()
                    extra[rows, cols] = more_target[...].astype(F32)

    def drain(half, first):
        for move in MOVES:
            @pl.when(inside(move, 1))
            def _(move=move):
                halo_copy(move, half).wait_send()
                if first:
                    extra_copy(move).wait_send()

    def advance(half, r):
        for i in range(r, ROWS - r):
            row = state[i]
            taps[i, :, 0:C] = pltpu.roll(row, 1, 0).astype(BF16)
            taps[i, :, C : 2 * C] = row.astype(BF16)
            taps[i, :, 2 * C : 3 * C] = pltpu.roll(row, COLS - 1, 0).astype(BF16)
        round_index = half * HALF + r
        lane = lax.broadcasted_iota(jnp.int32, (LANES, 2 * C), 0)
        chosen = ((lane < 32) & (lax.rem(lane, 16) // 2 == round_index)) | (lane >= 32)
        drive_now = jnp.where(chosen, drive[...], 0.0).astype(BF16)
        low, high = r + 1, ROWS - 1 - r
        width = COLS if r < HALF - 1 else 32
        count = (high - low) * width
        candidate = dot(
            extra_low[low:high, 0:width].reshape(count, LANES), drive_now[:, 0:C]
        )
        for a in range(3):
            candidate += dot(
                taps[low + a - 1 : high + a - 1, 0:width].reshape(count, 3 * C),
                conv_w[3 * a : 3 * a + 3].reshape(3 * C, C),
            )
        gate = dot(
            taps[low:high, 0:width, C : 2 * C].reshape(count, C), gate_w[...]
        ) + dot(extra_low[low:high, 0:width].reshape(count, LANES), drive_now[:, C : 2 * C])
        update = 0.5 + 0.5 * jnp.tanh(0.5 * gate)
        before = state[low:high, 0:width].reshape(count, C)
        after = before + update * (jnp.tanh(candidate) - before)
        after = after.reshape(high - low, width, C)
        if r == HALF - 1:
            state[low:high, 0:width] = after
        else:
            for i in range(low, high):
                keep = column_inside
                if i < 4:
                    keep = keep & (g > 0)
                if i >= 12:
                    keep = keep & (g < ctx_size - 1)
                state[i] = jnp.where(keep, after[i - low], 0.0)

    def tile_copy(phase, step, source, target):
        return pltpu.make_async_remote_copy(
            src_ref=source,
            dst_ref=target,
            send_sem=tile_send.at[phase, step],
            recv_sem=tile_recv.at[phase, step],
            device_id=(g, lax.rem(t + step, tile_size)),
            device_id_type=MESH,
        )

    def ctx_copy(step, source, target):
        return pltpu.make_async_remote_copy(
            src_ref=source,
            dst_ref=target,
            send_sem=ctx_send.at[step],
            recv_sem=ctx_recv.at[step],
            device_id=(lax.rem(g + step, ctx_size), t),
            device_id_type=MESH,
        )

    def context():
        pooled = []
        for i in range(4, 12, 2):
            pair = state[i, 0:32] + state[i + 1, 0:32]
            pooled.append(((pair + pltpu.roll(pair, 31, 0)) * 0.25).astype(BF16))
        pooled = jnp.concatenate(pooled, axis=0)
        assign = jnp.concatenate(
            [extra[i, 0:32, ASSIGN : ASSIGN + 1] for i in range(4, 12, 2)], axis=0
        )
        even = lax.rem(lax.broadcasted_iota(jnp.int32, (128, 128), 0), 2) == 0
        token = lax.broadcasted_iota(jnp.int32, (128, 128), 1).astype(F32)
        member = ((assign == token) & even).astype(F32).astype(BF16)
        partial = lax.dot_general(
            member, pooled, (((0,), (0,)), ((), ())), preferred_element_type=F32
        )
        partial_send[...] = partial.reshape(tile_size, 8, C).astype(BF16)
        partial_recv[0] = partial_send[t]
        for step in range(1, tile_size):
            tile_copy(
                0, step, partial_send.at[lax.rem(t + step, tile_size)], partial_recv.at[step]
            ).start()
        total = partial_recv[0].astype(F32)
        for step in range(1, tile_size):
            tile_copy(0, step, partial_send.at[0], partial_recv.at[step]).wait_recv()
            total += partial_recv[step].astype(F32)
        summed_all[t] = total.astype(BF16)
        for step in range(1, tile_size):
            tile_copy(1, step, summed_all.at[t], summed_all.at[t]).start()
        for step in range(1, tile_size):
            sender = lax.rem(t + tile_size - step, tile_size)
            tile_copy(1, step, summed_all.at[t], summed_all.at[sender]).wait_recv()
        for copy in weight_copies[2:7]:
            copy.wait()
        summed = summed_all[...].reshape(128, C)
        tokens = embed_w[...].astype(F32) + dot(summed, pool_w[...])
        normed = rms_norm(tokens, attn_norm_gain[...]).astype(BF16)
        queries[...] = dot(normed, qkv_w[0])
        keys_values[g, 0] = dot(normed, qkv_w[1]).astype(BF16)
        keys_values[g, 1] = dot(normed, qkv_w[2]).astype(BF16)
        for step in range(1, ctx_size):
            ctx_copy(step, keys_values.at[g], keys_values.at[g]).start()
        for step in range(1, ctx_size):
            sender = lax.rem(g + ctx_size - step, ctx_size)
            ctx_copy(step, keys_values.at[g], keys_values.at[sender]).wait_recv()
        query = queries[pl.ds(pl.multiple_of(part * 64, 64), 64)].astype(BF16)
        scores = jnp.concatenate(
            [
                lax.dot_general(
                    query,
                    keys_values[i, 0],
                    (((1,), (1,)), ((), ())),
                    preferred_element_type=F32,
                )
                for i in range(ctx_size)
            ],
            axis=1,
        ) * (1.0 / math.sqrt(HDIM))
        weights = jnp.exp(scores - jnp.max(scores, axis=-1, keepdims=True))
        denominator = jnp.sum(weights, axis=-1, keepdims=True)
        weights_low = weights.astype(BF16)
        weighted = jnp.zeros((64, HDIM), F32)
        for i in range(ctx_size):
            weighted += dot(weights_low[:, i * 128 : (i + 1) * 128], keys_values[i, 1])
        attention_all[t] = (weighted / denominator).astype(BF16)
        for step in range(1, tile_size):
            tile_copy(2, step, attention_all.at[t], attention_all.at[t]).start()
        for step in range(1, tile_size):
            sender = lax.rem(t + tile_size - step, tile_size)
            tile_copy(2, step, attention_all.at[t], attention_all.at[sender]).wait_recv()
        for i in range(tile_size):
            attention_full[
                (i % 2) * 64 : (i % 2) * 64 + 64, (i // 2) * HDIM : (i // 2 + 1) * HDIM
            ] = attention_all[i]
        for copy in weight_copies[7:]:
            copy.wait()
        attended = tokens + dot(attention_full[...], out_w[...])
        mlp_in = rms_norm(attended, mlp_norm_gain[...]).astype(BF16)
        hidden = jax.nn.gelu(dot(mlp_in, up_w[...])).astype(BF16)
        context = (attended + dot(hidden, down_w[...])).astype(BF16)
        context_out[...] = context
        returned = dot(context, return_w[...])
        returned_high = returned.astype(BF16)
        returned_low = (returned - returned_high.astype(F32)).astype(BF16)
        assign = extra[OWN_ROWS, 0:32, ASSIGN : ASSIGN + 1].reshape(256, 1)
        member = (
            (assign == lax.broadcasted_iota(jnp.int32, (256, 128), 1).astype(F32))
            .astype(F32)
            .astype(BF16)
        )
        share = dot(member, returned_high) + dot(member, returned_low)
        after = state[OWN_ROWS, 0:32] + share.reshape(8, 32, C)
        state[OWN_ROWS, 0:32] = after
        low = after.astype(BF16)
        edge_ns[1] = low
        edge_ew[1, 0] = after[:, 0:8].astype(BF16)
        edge_ew[1, 1] = after[:, 24:32].astype(BF16)
        for step in range(1, tile_size):
            tile_copy(0, step, partial_send.at[0], partial_recv.at[step]).wait_send()
            tile_copy(1, step, summed_all.at[t], summed_all.at[t]).wait_send()
            tile_copy(2, step, attention_all.at[t], attention_all.at[t]).wait_send()
        for step in range(1, ctx_size):
            ctx_copy(step, keys_values.at[g], keys_values.at[g]).wait_send()

    def half_window(half, _):
        @pl.when(half == 0)
        def _():
            for copy in edge_copies:
                copy.wait()
            exchange(0, True)
            extra_low[...] = extra[...].astype(BF16)
            weight_copies[0].wait()
            weight_copies[1].wait()
            drain(0, True)

        @pl.when(half == 1)
        def _():
            context()
            exchange(1, False)
            drain(1, False)

        for r in range(HALF):
            advance(half, r)
        return 0

    lax.fori_loop(0, 2, half_window, 0)
    state_out[...] = state[OWN_ROWS, 0:32].astype(BF16)


def local(
    syndrome_bits,
    region_assign,
    state_in,
    bit_to_candidate,
    bit_to_gate,
    conv_weight,
    gate_weight,
    gate_bias,
    pool_weight,
    region_embed,
    attn_norm_gain,
    query_weight,
    key_weight,
    value_weight,
    out_weight,
    mlp_norm_gain,
    mlp_up,
    mlp_down,
    return_weight,
):
    rows, cols = state_in.shape[0], state_in.shape[1]
    bits = syndrome_bits.transpose(2, 3, 0, 1).reshape(rows, cols, 2 * ROUNDS)
    assign = jnp.broadcast_to(
        region_assign[:, None, :, None], (rows // 2, 2, cols // 2, 2)
    ).reshape(rows, cols, 1)
    ones = jnp.ones((rows, cols, 2), jnp.int32)
    extra = jnp.concatenate(
        [
            bits,
            bits,
            ones,
            jnp.zeros((rows, cols, ASSIGN - 34), jnp.int32),
            assign,
            jnp.zeros((rows, cols, LANES - ASSIGN - 1), jnp.int32),
        ],
        axis=-1,
    ).astype(BF16)
    vmem = pl.BlockSpec(memory_space=pltpu.VMEM)
    hbm = pl.BlockSpec(memory_space=pl.ANY)
    dma = pltpu.SemaphoreType.DMA
    return pl.pallas_call(
        window,
        out_shape=(
            jax.ShapeDtypeStruct((rows, cols, C), BF16),
            jax.ShapeDtypeStruct((128, E), BF16),
        ),
        in_specs=[
            hbm, hbm, vmem, vmem, hbm, hbm, vmem, hbm, hbm, vmem,
            hbm, hbm, hbm, hbm, vmem, hbm, hbm, hbm,
        ],
        out_specs=(vmem, vmem),
        scratch_shapes=[
            pltpu.VMEM((ROWS, COLS, C), F32),
            pltpu.VMEM((ROWS, COLS, 3 * C), BF16),
            pltpu.VMEM((ROWS, COLS, LANES), F32),
            pltpu.VMEM((ROWS, COLS, LANES), BF16),
            pltpu.VMEM((LANES, 2 * C), F32),
            pltpu.VMEM((9, C, C), BF16),
            pltpu.VMEM((C, C), BF16),
            pltpu.VMEM((C, E), BF16),
            pltpu.VMEM((128, E), BF16),
            pltpu.VMEM((3, E, HDIM), BF16),
            pltpu.VMEM((E, E), BF16),
            pltpu.VMEM((E, 2 * E), BF16),
            pltpu.VMEM((2 * E, E), BF16),
            pltpu.VMEM((E, C), BF16),
            pltpu.VMEM((2, 8, 32, C), BF16),
            pltpu.VMEM((2, 2, 8, 8, C), BF16),
            pltpu.VMEM((8, 32, LANES), BF16),
            pltpu.VMEM((2, 8, 8, LANES), BF16),
            pltpu.VMEM((2, 2, 4, 32, C), BF16),
            pltpu.VMEM((2, 2, 8, 8, C), BF16),
            pltpu.VMEM((2, 4, 4, 8, C), BF16),
            pltpu.VMEM((2, 4, 32, LANES), BF16),
            pltpu.VMEM((2, 8, 8, LANES), BF16),
            pltpu.VMEM((4, 4, 8, LANES), BF16),
            pltpu.VMEM((16, 8, C), BF16),
            pltpu.VMEM((16, 8, C), BF16),
            pltpu.VMEM((16, 8, C), BF16),
            pltpu.VMEM((128, HDIM), F32),
            pltpu.VMEM((8, 2, 128, HDIM), BF16),
            pltpu.VMEM((16, 64, HDIM), BF16),
            pltpu.VMEM((128, E), BF16),
            dma((11,)),
            dma((6,)),
            dma((3, 8)),
            dma((3, 8)),
            dma((3, 16)),
            dma((3, 16)),
            dma((8,)),
            dma((8,)),
        ],
        compiler_params=pltpu.CompilerParams(
            collective_id=0, has_side_effects=True, vmem_limit_bytes=60 << 20
        ),
        name="window",
    )(
        extra,
        state_in,
        bit_to_candidate,
        bit_to_gate,
        conv_weight,
        gate_weight,
        gate_bias.reshape(1, -1),
        pool_weight,
        region_embed,
        attn_norm_gain.reshape(1, -1),
        query_weight,
        key_weight,
        value_weight,
        out_weight,
        mlp_norm_gain.reshape(1, -1),
        mlp_up,
        mlp_down,
        return_weight,
    )


def solution(mesh):
    return jax.shard_map(
        local,
        mesh=mesh,
        in_specs=(
            P(None, None, "ctx", "tile"),
            P("ctx", "tile"),
            P("ctx", "tile", None),
            P(),
            P(),
            P(),
            P(),
            P(),
            P(),
            P("ctx", None),
            P(),
            P(),
            P(),
            P(),
            P(),
            P(),
            P(),
            P(),
            P(),
        ),
        out_specs=(P("ctx", "tile", None), P("ctx", None)),
        check_vma=False,
    )
```

time: 694 us -> 91.6 us (0.13)
  waiting for transfers between devices: 487 us -> 0 us
  starting transfers between devices: 113 us -> 0 us
  Pallas kernels: 0 us -> 84.1 us
  matrix products: 39.9 us -> 0 us
  blocking collectives: 18 us -> 0 us
  between operations: 15.2 us -> 0.67 us
    all_gather x2 -> x0, waiting for transfers between devices: 388 us -> none  [the longest x1 194 us: gather_split(): lax.all_gather(key_rows, ('ctx', 'tile'), axis=0, tiled=True)]
    ppermute x32 -> x0, starting transfers between devices: 113 us -> none  [the longest x16 78 us: extended(): after = lax.ppermute(first, axis, down)]
    pallas_call x0 -> x1, Pallas kernels: none -> 84.1 us  [local(): pl.pallas_call(window, out_shape=(jax.ShapeDtypeStruct((rows, cols, C), B...]
    reduce_scatter x1 -> x0, waiting for transfers between devices: 63.2 us -> none  [local(): lax.psum_scatter(partial_value.astype(jnp.bfloat16), 'tile', scatter_dime...]
    dot_general x25 -> x0, matrix products: 39.9 us -> none  [the longest x8 16.1 us: advance(): jnp.dot(columns.reshape(patch_rows * patch_cols, 9 * channels), conv_flat...]
    ppermute x32 -> x0, waiting for transfers between devices: 35.7 us -> none  [the longest x16 24.5 us: extended(): before = lax.ppermute(last, axis, up)]
    all_gather x1 -> x0, blocking collectives: 18 us -> none  [local(): context_out = lax.all_gather(local_context, 'tile', axis=0, tiled=True)]
  transfers between devices with their start and end apart: 35 -> 0, of which waited for: 19 -> 0; matrix products, arithmetic and copies ran while one was open for 1% -> 0% of each run, Pallas kernels for 0% -> 0%
where the time goes in v1:
time: 91.6 us; the launch traced here: 90.8 us
  Pallas kernels  84.1 us (92%)
  local copies, waits for them, and re-layouts  4.46 us (5%)
  other arithmetic  1.53 us (2%)
    pallas_call x1, Pallas kernels, local(): pl.pallas_call(window, out_shape=(jax.ShapeDtypeStruct((rows, cols, C), B...  84.1 us
    unnamed x2, local copies, waits for them, and re-layouts  3.34 us

profile of v1, /device:TPU:6, one launch (start us, length us, event | category | flops | bytes accessed | tf_op | source)
XLA Modules:
  0.0 90.8 jit_solution(5006234340363048949)
XLA Ops:
  0.6 0.7 convert.16
  1.3 0.1 broadcast_in_dim.17
  1.4 0.1 reshape.27
  1.5 0.8 convert.18
  2.3 0.1 copy.22
  2.5 0.8 concatenate.4.extra_in
  3.3 84.1 %window.1 = (bf16[8,32,512]{2,1,0:T(8,128)(2,1)}, bf16[128,1024]{1,0:T(8,128)(2,1)}) custom-call(bf16[8,32,128]{2,1,0:T(8,128)(2,1)} %concatenate.4.extra_in, bf16[8,32,512]{2,1,0:T(8,128)(2,1)} %state_in.1, f32[2,512]{1,0:T(2,128)} %bit_to_candidate.1, f32[2,512]{1,0:T(2,128)} %bit_to_gate.1, bf16[9,512,512]{2,1,0:T(8,128)(2,1)} %conv_weight.1, ...), custom_call_target="tpu_custom_call" | custom-call | tf_op jit(solution)/shard_map/window/pallas_call | solution.py:493
  87.4 1.7 %copy.27 = bf16[8,32,512]{2,1,0:T(8,128)(2,1)} copy(bf16[8,32,512]{2,1,0:T(8,128)(2,1)} %get-tuple-element.4) | data formatting | bytes 524288
  89.1 1.7 %copy.28 = bf16[128,1024]{1,0:T(8,128)(2,1)} copy(bf16[128,1024]{1,0:T(8,128)(2,1)} %get-tuple-element.5) | data formatting | bytes 524288
  (3 shorter events, 0.0 us)

commit v2 on v1

v2 whole, which is shorter than its diff:
```python
import functools
import math

import jax
import jax.numpy as jnp
from jax import lax
from jax.experimental import pallas as pl
from jax.experimental.pallas import tpu as pltpu
from jax.sharding import PartitionSpec as P

MESH = pl.DeviceIdType.MESH
BF16 = jnp.bfloat16
F32 = jnp.float32

HEADS = 8
HDIM = 128
ROUNDS = 8
HALF = 4
C = 512
E = 1024
ROWS = 16
COLS = 48
OWN_ROWS = slice(4, 12)
LANES = 128
ASSIGN = 40

WIDE = C + LANES
BLOCKS = COLS // 2

MOVES = ((-1, 0), (1, 0), (0, -1), (0, 1), (-1, -1), (-1, 1), (1, -1), (1, 1))

TILE_STEPS = sorted(
    ((dz, dx, dc) for dz in range(4) for dx in range(2) for dc in range(2) if dz + dx + dc),
    key=lambda s: (-(min(s[0], 4 - s[0]) + s[1]), s),
)
CTX_STEPS = sorted(
    ((dx, dy) for dx in range(2) for dy in range(4) if dx + dy),
    key=lambda s: (-(2 * s[0] + min(s[1], 4 - s[1])), s),
)


def dot(left, right):
    return jnp.dot(left, right, preferred_element_type=F32)


def rms_norm(values, gain):
    return values * lax.rsqrt(jnp.mean(values * values, axis=-1, keepdims=True) + 1e-05) * gain


def window(
    syndrome_bits,
    region_assign,
    state_in,
    bit_to_candidate,
    bit_to_gate,
    conv_weight,
    gate_weight,
    gate_bias,
    pool_weight,
    region_embed,
    attn_norm_gain,
    query_weight,
    key_weight,
    value_weight,
    out_weight,
    mlp_norm_gain,
    mlp_up,
    mlp_down,
    return_weight,
    state_out,
    context_out,
    bits,
    assign_in,
    to_candidate,
    to_gate,
    bias_in,
    attn_gain,
    mlp_gain,
    state,
    taps,
    extra,
    extra_low,
    drive,
    conv_w,
    gate_w,
    pool_w,
    embed_w,
    qkv_w,
    out_w,
    up_w,
    down_w,
    return_w,
    first_ns,
    first_ew,
    first_halo_ns,
    first_halo_ew,
    first_halo_corner,
    edge_ns,
    edge_ew,
    halo_ns,
    halo_ew,
    halo_corner,
    partial_send,
    partial_recv,
    summed_all,
    queries,
    keys_values,
    attention_all,
    attention_full,
    member_cells,
    member_blocks,
    share_send,
    share_recv,
    small_sem,
    weight_sem,
    edge_sem,
    halo_send,
    halo_recv,
    tile_send,
    tile_recv,
    ctx_send,
    ctx_recv,
    relay_send,
    relay_recv,
    share_sems,
):
    g, t = lax.axis_index("ctx"), lax.axis_index("tile")
    ctx_size, tile_size = 8, 16
    head, part = t // 2, lax.rem(t, 2)

    def tile_peer(step, sign):
        dz, dx, dc = step
        z = lax.rem(t // 4 + (dz if sign > 0 else 4 - dz), 4)
        x = lax.rem(lax.rem(t // 2, 2) + dx, 2)
        core = lax.rem(t + dc, 2)
        return z * 4 + x * 2 + core

    def ctx_peer(step, sign):
        dx, dy = step
        x = lax.rem(g // 4 + dx, 2)
        y = lax.rem(g + (dy if sign > 0 else 4 - dy), 4)
        return x * 4 + y

    def inside(move, sign):
        dg, dt = move
        peer_g, peer_t = g + sign * dg, t + sign * dt
        return (peer_g >= 0) & (peer_g < ctx_size) & (peer_t >= 0) & (peer_t < tile_size)

    barrier = pltpu.get_barrier_semaphore()
    heard = jnp.int32(0)
    for move in MOVES[4:]:
        @pl.when(inside(move, 1))
        def _(move=move):
            pl.semaphore_signal(
                barrier, 1, device_id=(g + move[0], t + move[1]), device_id_type=MESH
            )
        heard += inside(move, -1).astype(jnp.int32)
    for step in CTX_STEPS:
        pl.semaphore_signal(barrier, 1, device_id=(ctx_peer(step, 1), t), device_id_type=MESH)
    for step in TILE_STEPS:
        pl.semaphore_signal(barrier, 1, device_id=(g, tile_peer(step, 1)), device_id_type=MESH)

    small_copies = [
        pltpu.make_async_copy(src, dst, small_sem.at[i])
        for i, (src, dst) in enumerate(
            (
                (syndrome_bits, bits),
                (region_assign, assign_in),
                (bit_to_candidate, to_candidate),
                (bit_to_gate, to_gate),
                (gate_bias, bias_in),
                (attn_norm_gain, attn_gain),
                (mlp_norm_gain, mlp_gain),
            )
        )
    ]
    edge_copies = [
        pltpu.make_async_copy(state_in, first_ns.at[:, :, 0:C], edge_sem.at[0]),
        pltpu.make_async_copy(state_in.at[:, 0:8], first_ew.at[0, :, :, 0:C], edge_sem.at[1]),
        pltpu.make_async_copy(state_in.at[:, 24:32], first_ew.at[1, :, :, 0:C], edge_sem.at[2]),
    ]
    head_cols = pl.ds(pl.multiple_of(head * HDIM, HDIM), HDIM)
    weight_copies = [
        pltpu.make_async_copy(src, dst, weight_sem.at[i])
        for i, (src, dst) in enumerate(
            (
                (conv_weight, conv_w),
                (gate_weight, gate_w),
                (pool_weight, pool_w),
                (region_embed, embed_w),
                (query_weight.at[:, head_cols], qkv_w.at[0]),
                (key_weight.at[:, head_cols], qkv_w.at[1]),
                (value_weight.at[:, head_cols], qkv_w.at[2]),
                (out_weight, out_w),
                (mlp_up, up_w),
                (mlp_down, down_w),
                (return_weight, return_w),
            )
        )
    ]
    for copy in small_copies + edge_copies + weight_copies:
        copy.start()

    state[...] = jnp.zeros_like(state)
    extra[...] = jnp.zeros_like(extra)
    for copy in small_copies:
        copy.wait()

    flat = bits[...].reshape(2 * ROUNDS * 8, 32).astype(F32).astype(BF16)
    source = lax.broadcasted_iota(jnp.int32, (128, 8 * LANES), 0)
    place_to = lax.broadcasted_iota(jnp.int32, (128, 8 * LANES), 1)
    target_row, target_lane = place_to // LANES, lax.rem(place_to, LANES)
    spread = (
        (lax.rem(source, 8) == target_row)
        & (target_lane < 32)
        & (lax.rem(target_lane, 16) == source // 8)
    )
    by_row = lax.dot_general(
        flat,
        spread.astype(F32).astype(BF16),
        (((0,), (0,)), ((), ())),
        preferred_element_type=F32,
    )
    block_of = (
        lax.broadcasted_iota(jnp.int32, (32, 16), 0) // 2
        == lax.broadcasted_iota(jnp.int32, (32, 16), 1)
    )
    assign_lane = (
        (lax.broadcasted_iota(jnp.int32, (16, LANES), 1) == ASSIGN).astype(F32).astype(BF16)
    )
    lane = lax.broadcasted_iota(jnp.int32, (32, LANES), 1)
    ones = ((lane == 32) | (lane == 33)).astype(F32)
    for i in range(8):
        tokens_of = jnp.where(
            block_of, assign_in[i // 2 : i // 2 + 1].astype(F32), 0.0
        ).astype(BF16)
        row = by_row[:, i * LANES : (i + 1) * LANES] + dot(tokens_of, assign_lane) + ones
        extra[4 + i, 0:32] = row
        first_ns[i, :, C:WIDE] = row.astype(BF16)
        first_ew[0, i, :, C:WIDE] = row[0:8].astype(BF16)
        first_ew[1, i, :, C:WIDE] = row[24:32].astype(BF16)

    lane_row = lax.broadcasted_iota(jnp.int32, (LANES, 2 * C), 0)
    both = jnp.concatenate([to_candidate[...], to_gate[...]], axis=1)
    bias = jnp.concatenate([jnp.zeros_like(bias_in[...]), bias_in[...]], axis=1)
    both_high = both.astype(BF16).astype(F32)
    both_low = both - both_high
    bias_high = bias.astype(BF16).astype(F32)
    bias_low = bias - bias_high
    even_row = lax.rem(lane_row, 2) == 0
    drive[...] = jnp.where(
        lane_row < 16,
        jnp.where(even_row, both_high[0:1], both_high[1:2]),
        jnp.where(
            lane_row < 32,
            jnp.where(even_row, both_low[0:1], both_low[1:2]),
            jnp.where(
                lane_row == 32, bias_high, jnp.where(lane_row == 33, bias_low, 0.0)
            ),
        ),
    )

    column = lax.broadcasted_iota(jnp.int32, (COLS, 1), 0)
    column_inside = ~(
        ((t == 0) & (column >= 40))
        | ((t == tile_size - 1) & (column >= 32) & (column < 40))
    )

    def halo_parts(move, half):
        dg, dt = move
        index = MOVES.index(move)
        rows = {0: slice(0, 8), -1: slice(0, 4), 1: slice(4, 8)}[dg]
        side = 0 if dt == -1 else 1
        ns, ew = (edge_ns, edge_ew) if half else (first_ns, first_ew)
        if dt == 0:
            return ns.at[rows], (halo_ns if half else first_halo_ns).at[index]
        if dg == 0:
            return ew.at[side], (halo_ew if half else first_halo_ew).at[side]
        return ew.at[side, rows], (halo_corner if half else first_halo_corner).at[index - 4]

    def halo_copy(move, half):
        source, target = halo_parts(move, half)
        index = MOVES.index(move)
        return pltpu.make_async_remote_copy(
            src_ref=source,
            dst_ref=target,
            send_sem=halo_send.at[half, index],
            recv_sem=halo_recv.at[half, index],
            device_id=(g + move[0], t + move[1]),
            device_id_type=MESH,
        )

    def send_halos(half):
        for move in MOVES:
            @pl.when(inside(move, 1))
            def _(move=move):
                halo_copy(move, half).start()

    def drain_halos(half):
        for move in MOVES:
            @pl.when(inside(move, 1))
            def _(move=move):
                halo_copy(move, half).wait_send()

    def take_halos(moves, half):
        for move in moves:
            @pl.when(inside(move, -1))
            def _(move=move):
                dg, dt = move
                rows = {0: slice(4, 12), -1: slice(12, 16), 1: slice(0, 4)}[dg]
                cols = {0: slice(0, 32), -1: slice(32, 40), 1: slice(40, 48)}[dt]
                halo_copy(move, half).wait_recv()
                _, target = halo_parts(move, half)
                if half:
                    state[rows, cols] = target[...].astype(F32)
                else:
                    state[rows, cols] = target[:, :, 0:C].astype(F32)
                    extra[rows, cols] = target[:, :, C:WIDE].astype(F32)

    beside, beyond = MOVES[2:4], MOVES[0:2] + MOVES[4:8]

    def fill_taps(level, rows):
        for i in rows:
            row = state[i]
            taps[level, i, :, 0:C] = pltpu.roll(row, 1, 0).astype(BF16)
            taps[level, i, :, C : 2 * C] = row.astype(BF16)
            taps[level, i, :, 2 * C : 3 * C] = pltpu.roll(row, COLS - 1, 0).astype(BF16)

    def advance(half, level, spans, width):
        round_index = half * HALF + level
        lane = lax.broadcasted_iota(jnp.int32, (LANES, 2 * C), 0)
        chosen = ((lane < 32) & (lax.rem(lane, 16) // 2 == round_index)) | (lane >= 32)
        drive_now = jnp.where(chosen, drive[...], 0.0).astype(BF16)
        count = sum(high - low for low, high in spans) * width

        def cells(read):
            parts = [read(low, high) for low, high in spans]
            whole = parts[0] if len(parts) == 1 else jnp.concatenate(parts, axis=0)
            return whole.reshape(count, whole.shape[-1])

        flags = cells(lambda low, high: extra_low[low:high, 0:width])
        candidate = dot(flags, drive_now[:, 0:C])
        for a in range(3):
            candidate += dot(
                cells(lambda low, high: taps[level, low + a - 1 : high + a - 1, 0:width]),
                conv_w[3 * a : 3 * a + 3].reshape(3 * C, C),
            )
        gate = dot(
            cells(lambda low, high: taps[level, low:high, 0:width, C : 2 * C]), gate_w[...]
        ) + dot(flags, drive_now[:, C : 2 * C])
        update = 0.5 + 0.5 * jnp.tanh(0.5 * gate)
        before = cells(lambda low, high: state[low:high, 0:width])
        after = before + update * (jnp.tanh(candidate) - before)
        after = after.reshape(count // width, width, C)
        at = 0
        for low, high in spans:
            for i in range(low, high):
                if width < COLS:
                    state[i, 0:width] = after[at]
                else:
                    keep = column_inside
                    if i < 4:
                        keep = keep & (g > 0)
                    if i >= 12:
                        keep = keep & (g < ctx_size - 1)
                    state[i] = jnp.where(keep, after[at], 0.0)
                at += 1

    def tile_copy(phase, index, source, target):
        return pltpu.make_async_remote_copy(
            src_ref=source,
            dst_ref=target,
            send_sem=tile_send.at[phase, index],
            recv_sem=tile_recv.at[phase, index],
            device_id=(g, tile_peer(TILE_STEPS[index], 1)),
            device_id_type=MESH,
        )

    mine = pl.ds(pl.multiple_of(part * 64, 64), 64)

    def ctx_copy(index, owner):
        block = keys_values.at[owner, :, mine]
        return pltpu.make_async_remote_copy(
            src_ref=block,
            dst_ref=block,
            send_sem=ctx_send.at[index],
            recv_sem=ctx_recv.at[index],
            device_id=(ctx_peer(CTX_STEPS[index], 1), t),
            device_id_type=MESH,
        )

    def relay_copy(index, owner, which):
        block = keys_values.at[owner, :, which]
        return pltpu.make_async_remote_copy(
            src_ref=block,
            dst_ref=block,
            send_sem=relay_send.at[index],
            recv_sem=relay_recv.at[index],
            device_id=(g, t + 1 - 2 * part),
            device_id_type=MESH,
        )

    def share_copy(index):
        return pltpu.make_async_remote_copy(
            src_ref=share_send.at[index],
            dst_ref=share_recv.at[index],
            send_sem=share_sems.at[0, index],
            recv_sem=share_sems.at[1, index],
            device_id=(g + MOVES[index][0], t),
            device_id_type=MESH,
        )

    tile_steps, ctx_steps = range(len(TILE_STEPS)), range(len(CTX_STEPS))
    token_lane = lax.broadcasted_iota(jnp.int32, (128, 128), 1).astype(F32)

    def one_hot(tokens):
        count = tokens.shape[0]
        lanes = lax.broadcasted_iota(jnp.int32, (count, 128), 1).astype(F32)
        return (tokens == lanes).astype(F32).astype(BF16)

    def context():
        pooled = []
        for i in range(4, 12, 2):
            pair = state[i, 0:32] + state[i + 1, 0:32]
            pooled.append(((pair + pltpu.roll(pair, 31, 0)) * 0.25).astype(BF16))
        pooled = jnp.concatenate(pooled, axis=0)
        assign = jnp.concatenate(
            [extra[i, 0:32, ASSIGN : ASSIGN + 1] for i in range(4, 12, 2)], axis=0
        )
        even = lax.rem(lax.broadcasted_iota(jnp.int32, (128, 128), 0), 2) == 0
        member = ((assign == token_lane) & even).astype(F32).astype(BF16)
        partial = lax.dot_general(
            member, pooled, (((0,), (0,)), ((), ())), preferred_element_type=F32
        )
        partial_send[...] = partial.reshape(tile_size, 8, C).astype(BF16)
        for k in tile_steps:
            tile_copy(
                0, k, partial_send.at[tile_peer(TILE_STEPS[k], 1)], partial_recv.at[k]
            ).start()
        own = state[OWN_ROWS, 0:32]
        edge_ns[...] = own.astype(BF16)
        edge_ew[0] = own[:, 0:8].astype(BF16)
        edge_ew[1] = own[:, 24:32].astype(BF16)
        member_cells[...] = one_hot(
            extra[OWN_ROWS, :, ASSIGN : ASSIGN + 1].reshape(8 * COLS, 1)
        )
        pick = (
            (
                lax.broadcasted_iota(jnp.int32, (BLOCKS, COLS), 0) * 2
                == lax.broadcasted_iota(jnp.int32, (BLOCKS, COLS), 1)
            )
            .astype(F32)
            .astype(BF16)
        )
        for side in range(2):
            for k in range(2):
                tokens_of = dot(pick, extra_low[4 + 4 * side + 2 * k])[:, ASSIGN : ASSIGN + 1]
                member_blocks[side, k * BLOCKS : (k + 1) * BLOCKS] = one_hot(tokens_of)
        total = partial_send[t].astype(F32)
        for k in tile_steps:
            tile_copy(0, k, partial_send.at[0], partial_recv.at[k]).wait_recv()
            total += partial_recv[k].astype(F32)
        summed_all[t] = total.astype(BF16)
        for k in tile_steps:
            tile_copy(1, k, summed_all.at[t], summed_all.at[t]).start()
        for copy in weight_copies[2:7]:
            copy.wait()
        for k in tile_steps:
            sender = tile_peer(TILE_STEPS[k], -1)
            tile_copy(1, k, summed_all.at[t], summed_all.at[sender]).wait_recv()
        summed = summed_all[...].reshape(128, C)
        tokens = embed_w[...].astype(F32) + dot(summed, pool_w[...])
        normed = rms_norm(tokens, attn_gain[...]).astype(BF16)
        keys_values[g, 0] = dot(normed, qkv_w[1]).astype(BF16)
        keys_values[g, 1] = dot(normed, qkv_w[2]).astype(BF16)
        for k in ctx_steps:
            ctx_copy(k, g).start()
        queries[...] = dot(normed, qkv_w[0])
        other = pl.ds(pl.multiple_of((1 - part) * 64, 64), 64)
        for k in reversed(ctx_steps):
            sender = ctx_peer(CTX_STEPS[k], -1)
            ctx_copy(k, sender).wait_recv()
            relay_copy(k, sender, mine).start()
        for k in reversed(ctx_steps):
            relay_copy(k, ctx_peer(CTX_STEPS[k], -1), other).wait_recv()
        send_halos(1)
        query = queries[mine].astype(BF16)
        scores = jnp.concatenate(
            [
                lax.dot_general(
                    query,
                    keys_values[i, 0],
                    (((1,), (1,)), ((), ())),
                    preferred_element_type=F32,
                )
                for i in range(ctx_size)
            ],
            axis=1,
        ) * (1.0 / math.sqrt(HDIM))
        weights = jnp.exp(scores - jnp.max(scores, axis=-1, keepdims=True))
        denominator = jnp.sum(weights, axis=-1, keepdims=True)
        weights_low = weights.astype(BF16)
        weighted = dot(
            weights_low, jnp.concatenate([keys_values[i, 1] for i in range(ctx_size)], axis=0)
        )
        attention_all[t] = (weighted / denominator).astype(BF16)
        for k in tile_steps:
            tile_copy(2, k, attention_all.at[t], attention_all.at[t]).start()
        for copy in weight_copies[7:]:
            copy.wait()
        for k in tile_steps:
            sender = tile_peer(TILE_STEPS[k], -1)
            tile_copy(2, k, attention_all.at[t], attention_all.at[sender]).wait_recv()
        for i in range(tile_size):
            attention_full[
                (i % 2) * 64 : (i % 2) * 64 + 64, (i // 2) * HDIM : (i // 2 + 1) * HDIM
            ] = attention_all[i]
        attended = tokens + dot(attention_full[...], out_w[...])
        mlp_in = rms_norm(attended, mlp_gain[...]).astype(BF16)
        hidden = jax.nn.gelu(dot(mlp_in, up_w[...])).astype(BF16)
        context = (attended + dot(hidden, down_w[...])).astype(BF16)
        returned = dot(context, return_w[...])
        returned_high = returned.astype(BF16)
        for side in range(2):
            share_send[side] = (
                dot(member_blocks[side], returned_high).reshape(2, BLOCKS, C).astype(BF16)
            )
            @pl.when(inside(MOVES[side], 1))
            def _(side=side):
                share_copy(side).start()
        context_out[...] = context
        returned_low = (returned - returned_high.astype(F32)).astype(BF16)
        take_halos(beside, 1)
        share = dot(member_cells[...], returned_high) + dot(member_cells[...], returned_low)
        share = share.reshape(8, COLS, C)
        for i in range(8):
            state[4 + i] += jnp.where(column_inside, share[i], 0.0)

    def take_shares():
        take_halos(beyond, 1)
        unpick = (
            (
                lax.broadcasted_iota(jnp.int32, (COLS, BLOCKS), 0) // 2
                == lax.broadcasted_iota(jnp.int32, (COLS, BLOCKS), 1)
            )
            .astype(F32)
            .astype(BF16)
        )
        for side in range(2):
            @pl.when(inside(MOVES[side], -1))
            def _(side=side):
                share_copy(side).wait_recv()
                first = 12 if side == 0 else 0
                for k in range(2):
                    share = jnp.where(column_inside, dot(unpick, share_recv[side, k]), 0.0)
                    state[first + 2 * k] += share
                    state[first + 2 * k + 1] += share

    def half_window(half, _):
        @pl.when(half == 0)
        def _():
            for copy in edge_copies:
                copy.wait()
            pl.semaphore_wait(barrier, heard + (ctx_size - 1) + (tile_size - 1))
            send_halos(0)
            state[OWN_ROWS, 0:32] = first_ns[:, :, 0:C].astype(F32)
            take_halos(beside, 0)
            extra_low[OWN_ROWS] = extra[OWN_ROWS].astype(BF16)
            weight_copies[0].wait()
            weight_copies[1].wait()

        @pl.when(half == 1)
        def _():
            context()

        for level in range(HALF):
            fill_taps(level, range(4 + level, 12 - level))
            if level < HALF - 1:
                advance(half, level, ((5 + level, 11 - level),), COLS)

        @pl.when(half == 0)
        def _():
            take_halos(beyond, 0)
            extra_low[0:4] = extra[0:4].astype(BF16)
            extra_low[12:16] = extra[12:16].astype(BF16)

        @pl.when(half == 1)
        def _():
            take_shares()

        for level in range(HALF):
            fill_taps(level, (*range(level, 4 + level), *range(12 - level, 16 - level)))
            if level < HALF - 1:
                spans = ((1 + level, 5 + level), (11 - level, 15 - level))
                advance(half, level, spans, COLS)
            else:
                advance(half, level, ((4, 12),), 32)
        return 0

    lax.fori_loop(0, 2, half_window, 0)
    state_out[...] = state[OWN_ROWS, 0:32].astype(BF16)
    drain_halos(0)
    drain_halos(1)
    for k in tile_steps:
        tile_copy(0, k, partial_send.at[0], partial_recv.at[k]).wait_send()
        tile_copy(1, k, summed_all.at[t], summed_all.at[t]).wait_send()
        tile_copy(2, k, attention_all.at[t], attention_all.at[t]).wait_send()
    for k in ctx_steps:
        ctx_copy(k, g).wait_send()
        relay_copy(k, g, mine).wait_send()
    for side in range(2):
        @pl.when(inside(MOVES[side], 1))
        def _(side=side):
            share_copy(side).wait_send()


def local(
    syndrome_bits,
    region_assign,
    state_in,
    bit_to_candidate,
    bit_to_gate,
    conv_weight,
    gate_weight,
    gate_bias,
    pool_weight,
    region_embed,
    attn_norm_gain,
    query_weight,
    key_weight,
    value_weight,
    out_weight,
    mlp_norm_gain,
    mlp_up,
    mlp_down,
    return_weight,
):
    rows, cols = state_in.shape[0], state_in.shape[1]
    hbm = pl.BlockSpec(memory_space=pl.ANY)
    vmem = pl.BlockSpec(memory_space=pltpu.VMEM)
    dma = pltpu.SemaphoreType.DMA
    return pl.pallas_call(
        window,
        out_shape=(
            pltpu.VMEM((rows, cols, C), BF16),
            pltpu.VMEM((128, E), BF16),
        ),
        in_specs=[hbm] * 19,
        out_specs=(vmem, vmem),
        scratch_shapes=[
            pltpu.VMEM((ROUNDS, 2, 8, 32), jnp.int32),
            pltpu.VMEM((4, 16), jnp.int32),
            pltpu.VMEM((2, C), F32),
            pltpu.VMEM((2, C), F32),
            pltpu.VMEM((1, C), F32),
            pltpu.VMEM((1, E), F32),
            pltpu.VMEM((1, E), F32),
            pltpu.VMEM((ROWS, COLS, C), F32),
            pltpu.VMEM((HALF, ROWS, COLS, 3 * C), BF16),
            pltpu.VMEM((ROWS, COLS, LANES), F32),
            pltpu.VMEM((ROWS, COLS, LANES), BF16),
            pltpu.VMEM((LANES, 2 * C), F32),
            pltpu.VMEM((9, C, C), BF16),
            pltpu.VMEM((C, C), BF16),
            pltpu.VMEM((C, E), BF16),
            pltpu.VMEM((128, E), BF16),
            pltpu.VMEM((3, E, HDIM), BF16),
            pltpu.VMEM((E, E), BF16),
            pltpu.VMEM((E, 2 * E), BF16),
            pltpu.VMEM((2 * E, E), BF16),
            pltpu.VMEM((E, C), BF16),
            pltpu.VMEM((8, 32, WIDE), BF16),
            pltpu.VMEM((2, 8, 8, WIDE), BF16),
            pltpu.VMEM((2, 4, 32, WIDE), BF16),
            pltpu.VMEM((2, 8, 8, WIDE), BF16),
            pltpu.VMEM((4, 4, 8, WIDE), BF16),
            pltpu.VMEM((8, 32, C), BF16),
            pltpu.VMEM((2, 8, 8, C), BF16),
            pltpu.VMEM((2, 4, 32, C), BF16),
            pltpu.VMEM((2, 8, 8, C), BF16),
            pltpu.VMEM((4, 4, 8, C), BF16),
            pltpu.VMEM((16, 8, C), BF16),
            pltpu.VMEM((15, 8, C), BF16),
            pltpu.VMEM((16, 8, C), BF16),
            pltpu.VMEM((128, HDIM), F32),
            pltpu.VMEM((8, 2, 128, HDIM), BF16),
            pltpu.VMEM((16, 64, HDIM), BF16),
            pltpu.VMEM((128, E), BF16),
            pltpu.VMEM((8 * COLS, 128), BF16),
            pltpu.VMEM((2, 2 * BLOCKS, 128), BF16),
            pltpu.VMEM((2, 2, BLOCKS, C), BF16),
            pltpu.VMEM((2, 2, BLOCKS, C), BF16),
            dma((7,)),
            dma((11,)),
            dma((3,)),
            dma((2, 8)),
            dma((2, 8)),
            dma((3, 15)),
            dma((3, 15)),
            dma((7,)),
            dma((7,)),
            dma((7,)),
            dma((7,)),
            dma((2, 2)),
        ],
        compiler_params=pltpu.CompilerParams(
            collective_id=0, has_side_effects=True, vmem_limit_bytes=62 << 20
        ),
        name="window",
    )(
        syndrome_bits,
        region_assign,
        state_in,
        bit_to_candidate,
        bit_to_gate,
        conv_weight,
        gate_weight,
        gate_bias.reshape(1, -1),
        pool_weight,
        region_embed,
        attn_norm_gain.reshape(1, -1),
        query_weight,
        key_weight,
        value_weight,
        out_weight,
        mlp_norm_gain.reshape(1, -1),
        mlp_up,
        mlp_down,
        return_weight,
    )


def solution(mesh):
    return jax.shard_map(
        local,
        mesh=mesh,
        in_specs=(
            P(None, None, "ctx", "tile"),
            P("ctx", "tile"),
            P("ctx", "tile", None),
            P(),
            P(),
            P(),
            P(),
            P(),
            P(),
            P("ctx", None),
            P(),
            P(),
            P(),
            P(),
            P(),
            P(),
            P(),
            P(),
            P(),
        ),
        out_specs=(P("ctx", "tile", None), P("ctx", None)),
        check_vma=False,
    )
```

time: 91.6 us -> 77.6 us (0.85)
  Pallas kernels: 84.1 us -> 75.4 us
  local copies, waits for them, and re-layouts: 4.46 us -> 1.41 us
  other arithmetic: 1.53 us -> 0 us
    pallas_call x1, Pallas kernels: 84.1 us -> 75.4 us  [local(): pl.pallas_call(window, out_shape=(pltpu.VMEM((rows, cols, C), BF16), pltp...]
    unnamed x2, local copies, waits for them, and re-layouts: 3.34 us -> 1.41 us
    another operation x2 -> x0, other arithmetic: 1.53 us -> none
where the time goes in v2:
time: 77.6 us; the launch traced here: 77.5 us
  Pallas kernels  75.4 us (97%)
  local copies, waits for them, and re-layouts  1.41 us (2%)
    pallas_call x1, Pallas kernels, local(): pl.pallas_call(window, out_shape=(pltpu.VMEM((rows, cols, C), BF16), pltp...  75.4 us

profile of v2, /device:TPU:6, one launch (start us, length us, event | category | flops | bytes accessed | tf_op | source)
XLA Modules:
  0.0 77.5 jit_solution(16246100401404456623)
XLA Ops:
  0.6 75.4 %window.1 = (bf16[8,32,512]{2,1,0:T(8,128)(2,1)S(1)}, bf16[128,1024]{1,0:T(8,128)(2,1)S(1)}) custom-call(s32[8,2,8,32]{3,2,1,0:T(8,128)} %syndrome_bits.1, s32[4,16]{1,0:T(4,128)} %region_assign.1, bf16[8,32,512]{2,1,0:T(8,128)(2,1)} %state_in.1, f32[2,512]{1,0:T(2,128)} %bit_to_candidate.1, f32[2,512]{1,0:T(2,128)} %bit_to_gate.1, ...), custom_call_target="tpu_custom_call" | custom-call | tf_op jit(solution)/shard_map/window/pallas_call | solution.py:642
  76.1 0.7 copy.23
  76.8 0.7 copy.24

commit v3 on v2

--- a/solution.py
+++ b/solution.py
@@ -198,7 +198,7 @@
             )
         )
     ]
-    for copy in small_copies + edge_copies + weight_copies:
+    for copy in small_copies + edge_copies + weight_copies[:2]:
         copy.start()
 
     state[...] = jnp.zeros_like(state)
@@ -581,6 +581,8 @@
         @pl.when(half == 0)
         def _():
             take_halos(beyond, 0)
+            for copy in weight_copies[2:]:
+                copy.start()
             extra_low[0:4] = extra[0:4].astype(BF16)
             extra_low[12:16] = extra[12:16].astype(BF16)
 

time: 77.6 us -> 74.6 us (0.961)
  Pallas kernels: 75.4 us -> 72.4 us
    pallas_call x1, Pallas kernels: 75.4 us -> 72.4 us  [local(): pl.pallas_call(window, out_shape=(pltpu.VMEM((rows, cols, C), BF16), pltp...]
where the time goes in v3:
time: 74.6 us; the launch traced here: 74.5 us
  Pallas kernels  72.4 us (97%)
  local copies, waits for them, and re-layouts  1.41 us (2%)
    pallas_call x1, Pallas kernels, local(): pl.pallas_call(window, out_shape=(pltpu.VMEM((rows, cols, C), BF16), pltp...  72.4 us

profile of v3, /device:TPU:6, one launch (start us, length us, event | category | flops | bytes accessed | tf_op | source)
XLA Modules:
  0.0 74.5 jit_solution(23060550212203075)
XLA Ops:
  0.6 72.4 %window.1 = (bf16[8,32,512]{2,1,0:T(8,128)(2,1)S(1)}, bf16[128,1024]{1,0:T(8,128)(2,1)S(1)}) custom-call(s32[8,2,8,32]{3,2,1,0:T(8,128)} %syndrome_bits.1, s32[4,16]{1,0:T(4,128)} %region_assign.1, bf16[8,32,512]{2,1,0:T(8,128)(2,1)} %state_in.1, f32[2,512]{1,0:T(2,128)} %bit_to_candidate.1, f32[2,512]{1,0:T(2,128)} %bit_to_gate.1, ...), custom_call_target="tpu_custom_call" | custom-call | tf_op jit(solution)/shard_map/window/pallas_call | solution.py:644
  73.1 0.7 copy.23
  73.8 0.7 copy.24

commit v4 on v3

--- a/solution.py
+++ b/solution.py
@@ -19,13 +19,13 @@
 C = 512
 E = 1024
 ROWS = 16
-COLS = 48
+COLS = 40
 OWN_ROWS = slice(4, 12)
 LANES = 128
 ASSIGN = 40
 
 WIDE = C + LANES
-BLOCKS = COLS // 2
+BLOCKS = 24
 
 MOVES = ((-1, 0), (1, 0), (0, -1), (0, 1), (-1, -1), (-1, 1), (1, -1), (1, 1))
 
@@ -78,8 +78,10 @@
     mlp_gain,
     state,
     taps,
+    taps_beside,
     extra,
     extra_low,
+    extra_beside,
     drive,
     conv_w,
     gate_w,
@@ -176,8 +178,6 @@
     ]
     edge_copies = [
         pltpu.make_async_copy(state_in, first_ns.at[:, :, 0:C], edge_sem.at[0]),
-        pltpu.make_async_copy(state_in.at[:, 0:8], first_ew.at[0, :, :, 0:C], edge_sem.at[1]),
-        pltpu.make_async_copy(state_in.at[:, 24:32], first_ew.at[1, :, :, 0:C], edge_sem.at[2]),
     ]
     head_cols = pl.ds(pl.multiple_of(head * HDIM, HDIM), HDIM)
     weight_copies = [
@@ -230,6 +230,13 @@
     )
     lane = lax.broadcasted_iota(jnp.int32, (32, LANES), 1)
     ones = ((lane == 32) | (lane == 33)).astype(F32)
+    eight = lax.broadcasted_iota(jnp.int32, (8, 1), 0)
+
+    def pack(side, top, bottom):
+        keep = (eight < 4) if side == 0 else (eight >= 4)
+        return jnp.where(keep, top, pltpu.roll(bottom, 4, 0)).astype(BF16)
+
+    extra_rows = []
     for i in range(8):
         tokens_of = jnp.where(
             block_of, assign_in[i // 2 : i // 2 + 1].astype(F32), 0.0
@@ -237,8 +244,11 @@
         row = by_row[:, i * LANES : (i + 1) * LANES] + dot(tokens_of, assign_lane) + ones
         extra[4 + i, 0:32] = row
         first_ns[i, :, C:WIDE] = row.astype(BF16)
-        first_ew[0, i, :, C:WIDE] = row[0:8].astype(BF16)
-        first_ew[1, i, :, C:WIDE] = row[24:32].astype(BF16)
+        extra_rows.append(row)
+    for k in range(4):
+        top, bottom = extra_rows[2 * k], extra_rows[2 * k + 1]
+        first_ew[0, k, :, C:WIDE] = pack(0, top[0:8], bottom[0:8])
+        first_ew[1, k, :, C:WIDE] = pack(1, top[24:32], bottom[24:32])
 
     lane_row = lax.broadcasted_iota(jnp.int32, (LANES, 2 * C), 0)
     both = jnp.concatenate([to_candidate[...], to_gate[...]], axis=1)
@@ -262,21 +272,23 @@
 
     column = lax.broadcasted_iota(jnp.int32, (COLS, 1), 0)
     column_inside = ~(
-        ((t == 0) & (column >= 40))
-        | ((t == tile_size - 1) & (column >= 32) & (column < 40))
+        ((t == 0) & (column >= 36))
+        | ((t == tile_size - 1) & (column >= 32) & (column < 36))
     )
+    beside_inside = ~(((t == 0) & (eight >= 4)) | ((t == tile_size - 1) & (eight < 4)))
 
     def halo_parts(move, half):
         dg, dt = move
         index = MOVES.index(move)
         rows = {0: slice(0, 8), -1: slice(0, 4), 1: slice(4, 8)}[dg]
+        pairs = {-1: slice(0, 2), 1: slice(2, 4)}
         side = 0 if dt == -1 else 1
         ns, ew = (edge_ns, edge_ew) if half else (first_ns, first_ew)
         if dt == 0:
             return ns.at[rows], (halo_ns if half else first_halo_ns).at[index]
         if dg == 0:
             return ew.at[side], (halo_ew if half else first_halo_ew).at[side]
-        return ew.at[side, rows], (halo_corner if half else first_halo_corner).at[index - 4]
+        return ew.at[side, pairs[dg]], (halo_corner if half else first_halo_corner).at[index - 4]
 
     def halo_copy(move, half):
         source, target = halo_parts(move, half)
@@ -291,7 +303,7 @@
         )
 
     def send_halos(half):
-        for move in MOVES:
+        for move in MOVES[2:4] + MOVES[0:2] + MOVES[4:8]:
             @pl.when(inside(move, 1))
             def _(move=move):
                 halo_copy(move, half).start()
@@ -307,63 +319,98 @@
             @pl.when(inside(move, -1))
             def _(move=move):
                 dg, dt = move
-                rows = {0: slice(4, 12), -1: slice(12, 16), 1: slice(0, 4)}[dg]
-                cols = {0: slice(0, 32), -1: slice(32, 40), 1: slice(40, 48)}[dt]
+                first = {0: 4, -1: 12, 1: 0}[dg]
                 halo_copy(move, half).wait_recv()
                 _, target = halo_parts(move, half)
-                if half:
-                    state[rows, cols] = target[...].astype(F32)
-                else:
-                    state[rows, cols] = target[:, :, 0:C].astype(F32)
-                    extra[rows, cols] = target[:, :, C:WIDE].astype(F32)
+                if dt == 0:
+                    state[first : first + 4, 0:32] = target[:, :, 0:C].astype(F32)
+                    if not half:
+                        extra[first : first + 4, 0:32] = target[:, :, C:WIDE].astype(F32)
+                    return
+                here = (eight < 4) if dt == -1 else (eight >= 4)
+                for k in range(4 if dg == 0 else 2):
+                    for row in range(2):
+                        i = first + 2 * k + row
+                        parts = [(state, slice(0, C))]
+                        if not half:
+                            parts.append((extra, slice(C, WIDE)))
+                        for into, lanes in parts:
+                            came = target[k, :, lanes].astype(F32)
+                            if row:
+                                came = pltpu.roll(came, 4, 0)
+                            into[i, 32:40] = jnp.where(here, came, into[i, 32:40])
 
     beside, beyond = MOVES[2:4], MOVES[0:2] + MOVES[4:8]
 
     def fill_taps(level, rows):
         for i in rows:
             row = state[i]
-            taps[level, i, :, 0:C] = pltpu.roll(row, 1, 0).astype(BF16)
-            taps[level, i, :, C : 2 * C] = row.astype(BF16)
-            taps[level, i, :, 2 * C : 3 * C] = pltpu.roll(row, COLS - 1, 0).astype(BF16)
+            shifted = (pltpu.roll(row, 1, 0), row, pltpu.roll(row, COLS - 1, 0))
+            for k in range(3):
+                lanes = slice(k * C, (k + 1) * C)
+                taps[level, i, :, lanes] = shifted[k][0:32].astype(BF16)
+                taps_beside[level, i, :, lanes] = shifted[k][32:COLS].astype(BF16)
 
     def advance(half, level, spans, width):
         round_index = half * HALF + level
         lane = lax.broadcasted_iota(jnp.int32, (LANES, 2 * C), 0)
         chosen = ((lane < 32) & (lax.rem(lane, 16) // 2 == round_index)) | (lane >= 32)
         drive_now = jnp.where(chosen, drive[...], 0.0).astype(BF16)
-        count = sum(high - low for low, high in spans) * width
-
-        def cells(read):
+        lines = sum(high - low for low, high in spans)
+
+        def stack(read, columns):
             parts = [read(low, high) for low, high in spans]
             whole = parts[0] if len(parts) == 1 else jnp.concatenate(parts, axis=0)
-            return whole.reshape(count, whole.shape[-1])
-
-        flags = cells(lambda low, high: extra_low[low:high, 0:width])
+            return whole.reshape(lines * columns, whole.shape[-1])
+
+        def cells(own, halo):
+            if width < COLS:
+                return stack(own, 32)
+            return jnp.concatenate([stack(own, 32), stack(halo, COLS - 32)], axis=0)
+
+        flags = cells(
+            lambda low, high: extra_low[low:high], lambda low, high: extra_beside[low:high]
+        )
         candidate = dot(flags, drive_now[:, 0:C])
         for a in range(3):
             candidate += dot(
-                cells(lambda low, high: taps[level, low + a - 1 : high + a - 1, 0:width]),
+                cells(
+                    lambda low, high: taps[level, low + a - 1 : high + a - 1],
+                    lambda low, high: taps_beside[level, low + a - 1 : high + a - 1],
+                ),
                 conv_w[3 * a : 3 * a + 3].reshape(3 * C, C),
             )
         gate = dot(
-            cells(lambda low, high: taps[level, low:high, 0:width, C : 2 * C]), gate_w[...]
+            cells(
+                lambda low, high: taps[level, low:high, :, C : 2 * C],
+                lambda low, high: taps_beside[level, low:high, :, C : 2 * C],
+            ),
+            gate_w[...],
         ) + dot(flags, drive_now[:, C : 2 * C])
         update = 0.5 + 0.5 * jnp.tanh(0.5 * gate)
-        before = cells(lambda low, high: state[low:high, 0:width])
+        before = cells(
+            lambda low, high: state[low:high, 0:32], lambda low, high: state[low:high, 32:COLS]
+        )
         after = before + update * (jnp.tanh(candidate) - before)
-        after = after.reshape(count // width, width, C)
+        own = after[0 : lines * 32].reshape(lines, 32, C)
+        if width == COLS:
+            halo = after[lines * 32 :].reshape(lines, COLS - 32, C)
         at = 0
         for low, high in spans:
             for i in range(low, high):
-                if width < COLS:
-                    state[i, 0:width] = after[at]
+                if i < 4:
+                    there = g > 0
+                elif i >= 12:
+                    there = g < ctx_size - 1
                 else:
-                    keep = column_inside
-                    if i < 4:
-                        keep = keep & (g > 0)
-                    if i >= 12:
-                        keep = keep & (g < ctx_size - 1)
-                    state[i] = jnp.where(keep, after[at], 0.0)
+                    there = None
+                if there is None:
+                    state[i, 0:32] = own[at]
+                else:
+                    state[i, 0:32] = jnp.where(there, own[at], 0.0)
+                if width == COLS:
+                    keep = beside_inside if there is None else beside_inside & there
+                    state[i, 32:COLS] = jnp.where(keep, halo[at], 0.0)
                 at += 1
 
     def tile_copy(phase, index, source, target):
@@ -439,8 +486,9 @@
             ).start()
         own = state[OWN_ROWS, 0:32]
         edge_ns[...] = own.astype(BF16)
-        edge_ew[0] = own[:, 0:8].astype(BF16)
-        edge_ew[1] = own[:, 24:32].astype(BF16)
+        for k in range(4):
+            edge_ew[0, k] = pack(0, own[2 * k, 0:8], own[2 * k + 1, 0:8])
+            edge_ew[1, k] = pack(1, own[2 * k, 24:32], own[2 * k + 1, 24:32])
         member_cells[...] = one_hot(
             extra[OWN_ROWS, :, ASSIGN : ASSIGN + 1].reshape(8 * COLS, 1)
         )
@@ -454,7 +502,7 @@
         )
         for side in range(2):
             for k in range(2):
-                tokens_of = dot(pick, extra_low[4 + 4 * side + 2 * k])[:, ASSIGN : ASSIGN + 1]
+                tokens_of = dot(pick, extra[4 + 4 * side + 2 * k].astype(BF16))[:, ASSIGN : ASSIGN + 1]
                 member_blocks[side, k * BLOCKS : (k + 1) * BLOCKS] = one_hot(tokens_of)
         total = partial_send[t].astype(F32)
         for k in tile_steps:
@@ -556,16 +604,24 @@
                     state[first + 2 * k] += share
                     state[first + 2 * k + 1] += share
 
+    def keep_extra(low, high):
+        extra_low[low:high] = extra[low:high, 0:32].astype(BF16)
+        extra_beside[low:high] = extra[low:high, 32:COLS].astype(BF16)
+
     def half_window(half, _):
         @pl.when(half == 0)
         def _():
             for copy in edge_copies:
                 copy.wait()
+            state[OWN_ROWS, 0:32] = first_ns[:, :, 0:C].astype(F32)
+            for k in range(4):
+                top, bottom = 4 + 2 * k, 5 + 2 * k
+                first_ew[0, k, :, 0:C] = pack(0, state[top, 0:8], state[bottom, 0:8])
+                first_ew[1, k, :, 0:C] = pack(1, state[top, 24:32], state[bottom, 24:32])
             pl.semaphore_wait(barrier, heard + (ctx_size - 1) + (tile_size - 1))
             send_halos(0)
-            state[OWN_ROWS, 0:32] = first_ns[:, :, 0:C].astype(F32)
             take_halos(beside, 0)
-            extra_low[OWN_ROWS] = extra[OWN_ROWS].astype(BF16)
+            keep_extra(4, 12)
             weight_copies[0].wait()
             weight_copies[1].wait()
 
@@ -583,8 +639,8 @@
             take_halos(beyond, 0)
             for copy in weight_copies[2:]:
                 copy.start()
-            extra_low[0:4] = extra[0:4].astype(BF16)
-            extra_low[12:16] = extra[12:16].astype(BF16)
+            keep_extra(0, 4)
+            keep_extra(12, 16)
 
         @pl.when(half == 1)
         def _():
@@ -658,9 +714,11 @@
             pltpu.VMEM((1, E), F32),
             pltpu.VMEM((1, E), F32),
             pltpu.VMEM((ROWS, COLS, C), F32),
-            pltpu.VMEM((HALF, ROWS, COLS, 3 * C), BF16),
+            pltpu.VMEM((HALF, ROWS, 32, 3 * C), BF16),
+            pltpu.VMEM((HALF, ROWS, COLS - 32, 3 * C), BF16),
             pltpu.VMEM((ROWS, COLS, LANES), F32),
-            pltpu.VMEM((ROWS, COLS, LANES), BF16),
+            pltpu.VMEM((ROWS, 32, LANES), BF16),
+            pltpu.VMEM((ROWS, COLS - 32, LANES), BF16),
             pltpu.VMEM((LANES, 2 * C), F32),
             pltpu.VMEM((9, C, C), BF16),
             pltpu.VMEM((C, C), BF16),
@@ -672,15 +730,15 @@
             pltpu.VMEM((2 * E, E), BF16),
             pltpu.VMEM((E, C), BF16),
             pltpu.VMEM((8, 32, WIDE), BF16),
-            pltpu.VMEM((2, 8, 8, WIDE), BF16),
+            pltpu.VMEM((2, 4, 8, WIDE), BF16),
             pltpu.VMEM((2, 4, 32, WIDE), BF16),
-            pltpu.VMEM((2, 8, 8, WIDE), BF16),
-            pltpu.VMEM((4, 4, 8, WIDE), BF16),
+            pltpu.VMEM((2, 4, 8, WIDE), BF16),
+            pltpu.VMEM((4, 2, 8, WIDE), BF16),
             pltpu.VMEM((8, 32, C), BF16),
-            pltpu.VMEM((2, 8, 8, C), BF16),
+            pltpu.VMEM((2, 4, 8, C), BF16),
             pltpu.VMEM((2, 4, 32, C), BF16),
-            pltpu.VMEM((2, 8, 8, C), BF16),
-            pltpu.VMEM((4, 4, 8, C), BF16),
+            pltpu.VMEM((2, 4, 8, C), BF16),
+            pltpu.VMEM((4, 2, 8, C), BF16),
             pltpu.VMEM((16, 8, C), BF16),
             pltpu.VMEM((15, 8, C), BF16),
             pltpu.VMEM((16, 8, C), BF16),
@@ -694,7 +752,7 @@
             pltpu.VMEM((2, 2, BLOCKS, C), BF16),
             dma((7,)),
             dma((11,)),
-            dma((3,)),
+            dma((1,)),
             dma((2, 8)),
             dma((2, 8)),
             dma((3, 15)),

time: 74.6 us -> 67.6 us (0.906)
  Pallas kernels: 72.4 us -> 65.4 us
    pallas_call x1, Pallas kernels: 72.4 us -> 65.4 us  [local(): pl.pallas_call(window, out_shape=(pltpu.VMEM((rows, cols, C), BF16), pltp...]
where the time goes in v4:
time: 67.6 us; the launch traced here: 67.5 us
  Pallas kernels  65.4 us (97%)
  local copies, waits for them, and re-layouts  1.41 us (2%)
    pallas_call x1, Pallas kernels, local(): pl.pallas_call(window, out_shape=(pltpu.VMEM((rows, cols, C), BF16), pltp...  65.4 us
    unnamed x2, local copies, waits for them, and re-layouts  1.41 us

profile of v4, /device:TPU:6, one launch (start us, length us, event | category | flops | bytes accessed | tf_op | source)
XLA Modules:
  0.0 67.5 jit_solution(14811909927977191856)
XLA Ops:
  0.6 65.4 %window.1 = (bf16[8,32,512]{2,1,0:T(8,128)(2,1)S(1)}, bf16[128,1024]{1,0:T(8,128)(2,1)S(1)}) custom-call(s32[8,2,8,32]{3,2,1,0:T(8,128)} %syndrome_bits.1, s32[4,16]{1,0:T(4,128)} %region_assign.1, bf16[8,32,512]{2,1,0:T(8,128)(2,1)} %state_in.1, f32[2,512]{1,0:T(2,128)} %bit_to_candidate.1, f32[2,512]{1,0:T(2,128)} %bit_to_gate.1, ...), custom_call_target="tpu_custom_call" | custom-call | tf_op jit(solution)/shard_map/window/pallas_call | solution.py:700
  66.1 0.7 %copy.23 = bf16[8,32,512]{2,1,0:T(8,128)(2,1)} copy(bf16[8,32,512]{2,1,0:T(8,128)(2,1)S(1)} %get-tuple-element.2) | data formatting | bytes 524288
  66.8 0.7 %copy.24 = bf16[128,1024]{1,0:T(8,128)(2,1)} copy(bf16[128,1024]{1,0:T(8,128)(2,1)S(1)} %get-tuple-element.3) | data formatting | bytes 524288

commit v5 on v4

--- a/solution.py
+++ b/solution.py
@@ -519,7 +519,7 @@
         summed = summed_all[...].reshape(128, C)
         tokens = embed_w[...].astype(F32) + dot(summed, pool_w[...])
         normed = rms_norm(tokens, attn_gain[...]).astype(BF16)
-        keys_values[g, 0] = dot(normed, qkv_w[1]).astype(BF16)
+        keys_values[g, 0] = dot(normed, qkv_w[1]).T.astype(BF16)
         keys_values[g, 1] = dot(normed, qkv_w[2]).astype(BF16)
         for k in ctx_steps:
             ctx_copy(k, g).start()
@@ -531,19 +531,9 @@
             relay_copy(k, sender, mine).start()
         for k in reversed(ctx_steps):
             relay_copy(k, ctx_peer(CTX_STEPS[k], -1), other).wait_recv()
-        send_halos(1)
         query = queries[mine].astype(BF16)
-        scores = jnp.concatenate(
-            [
-                lax.dot_general(
-                    query,
-                    keys_values[i, 0],
-                    (((1,), (1,)), ((), ())),
-                    preferred_element_type=F32,
-                )
-                for i in range(ctx_size)
-            ],
-            axis=1,
+        scores = dot(
+            query, jnp.concatenate([keys_values[i, 0] for i in range(ctx_size)], axis=1)
         ) * (1.0 / math.sqrt(HDIM))
         weights = jnp.exp(scores - jnp.max(scores, axis=-1, keepdims=True))
         denominator = jnp.sum(weights, axis=-1, keepdims=True)
@@ -559,6 +549,7 @@
         for k in tile_steps:
             sender = tile_peer(TILE_STEPS[k], -1)
             tile_copy(2, k, attention_all.at[t], attention_all.at[sender]).wait_recv()
+        send_halos(1)
         for i in range(tile_size):
             attention_full[
                 (i % 2) * 64 : (i % 2) * 64 + 64, (i // 2) * HDIM : (i // 2 + 1) * HDIM
@@ -670,6 +661,17 @@
         @pl.when(inside(MOVES[side], 1))
         def _(side=side):
             share_copy(side).wait_send()
+
+
+def put_out(state_low, context, state_out, context_out, sems):
+    copies = [
+        pltpu.make_async_copy(state_low, state_out, sems.at[0]),
+        pltpu.make_async_copy(context, context_out, sems.at[1]),
+    ]
+    for copy in copies:
+        copy.start()
+    for copy in copies:
+        copy.wait()
 
 
 def local(
@@ -697,7 +699,7 @@
     hbm = pl.BlockSpec(memory_space=pl.ANY)
     vmem = pl.BlockSpec(memory_space=pltpu.VMEM)
     dma = pltpu.SemaphoreType.DMA
-    return pl.pallas_call(
+    state_low, context = pl.pallas_call(
         window,
         out_shape=(
             pltpu.VMEM((rows, cols, C), BF16),
@@ -788,6 +790,17 @@
         mlp_down,
         return_weight,
     )
+    return pl.pallas_call(
+        put_out,
+        out_shape=(
+            jax.ShapeDtypeStruct(state_low.shape, BF16),
+            jax.ShapeDtypeStruct(context.shape, BF16),
+        ),
+        in_specs=[vmem, vmem],
+        out_specs=(hbm, hbm),
+        scratch_shapes=[dma((2,))],
+        name="put_out",
+    )(*(pltpu.with_memory_space_constraint(x, pltpu.VMEM) for x in (state_low, context)))
 
 
 def solution(mesh):

time: 67.6 us -> 64.8 us (0.959)
  Pallas kernels: 65.4 us -> 63.6 us
  local copies, waits for them, and re-layouts: 1.41 us -> 0 us
    pallas_call x1, Pallas kernels: 65.4 us -> 62.8 us  [local(): pl.pallas_call(window, out_shape=(pltpu.VMEM((rows, cols, C), BF16), pltp...]
    unnamed x2 -> x0, local copies, waits for them, and re-layouts: 1.41 us -> none
    pallas_call x0 -> x1, Pallas kernels: none -> 0.81 us  [local(): pl.pallas_call(put_out, out_shape=(jax.ShapeDtypeStruct(state_low.shape,...]
where the time goes in v5:
time: 64.8 us; the launch traced here: 64.3 us
  Pallas kernels  63.6 us (98%)
  between operations  0.65 us (1%)
    pallas_call x1, Pallas kernels, local(): pl.pallas_call(window, out_shape=(pltpu.VMEM((rows, cols, C), BF16), pltp...  62.8 us

profile of v5, /device:TPU:6, one launch (start us, length us, event | category | flops | bytes accessed | tf_op | source)
XLA Modules:
  0.0 64.3 jit_solution(10397153922372989861)
XLA Ops:
  0.6 62.8 %window.1 = (bf16[8,32,512]{2,1,0:T(8,128)(2,1)S(1)}, bf16[128,1024]{1,0:T(8,128)(2,1)S(1)}) custom-call(s32[8,2,8,32]{3,2,1,0:T(8,128)} %syndrome_bits.1, s32[4,16]{1,0:T(4,128)} %region_assign.1, bf16[8,32,512]{2,1,0:T(8,128)(2,1)} %state_in.1, f32[2,512]{1,0:T(2,128)} %bit_to_candidate.1, f32[2,512]{1,0:T(2,128)} %bit_to_gate.1, ...), custom_call_target="tpu_custom_call" | custom-call | tf_op jit(solution)/shard_map/window/pallas_call | solution.py:702
  63.5 0.8 %put_out.1 = (bf16[8,32,512]{2,1,0:T(8,128)(2,1)}, bf16[128,1024]{1,0:T(8,128)(2,1)}) custom-call(bf16[8,32,512]{2,1,0:T(8,128)(2,1)S(1)} %get-tuple-element.4.state_low, bf16[128,1024]{1,0:T(8,128)(2,1)S(1)} %get-tuple-element.5.context), custom_call_target="tpu_custom_call" | custom-call | tf_op jit(solution)/shard_map/put_out/pallas_call | solution.py:793

commit v6 on v5

--- a/solution.py
+++ b/solution.py
@@ -628,14 +628,17 @@
         @pl.when(half == 0)
         def _():
             take_halos(beyond, 0)
-            for copy in weight_copies[2:]:
-                copy.start()
             keep_extra(0, 4)
             keep_extra(12, 16)
 
         @pl.when(half == 1)
         def _():
             take_shares()
+
+        @pl.when(half == 0)
+        def _():
+            for copy in weight_copies[2:]:
+                copy.start()
 
         for level in range(HALF):
             fill_taps(level, (*range(level, 4 + level), *range(12 - level, 16 - level)))

time: 64.8 us -> 64.8 us (level)
  no operation moved by 1% of the time
where the time goes in v6:
time: 64.8 us; the launch traced here: 64.3 us
  Pallas kernels  63.6 us (98%)
  between operations  0.65 us (1%)
    pallas_call x1, Pallas kernels, local(): pl.pallas_call(window, out_shape=(pltpu.VMEM((rows, cols, C), BF16), pltp...  62.8 us

profile of v6, /device:TPU:6, one launch (start us, length us, event | category | flops | bytes accessed | tf_op | source)
XLA Modules:
  0.0 64.3 jit_solution(11789854190324876744)
XLA Ops:
  0.6 62.8 %window.1 = (bf16[8,32,512]{2,1,0:T(8,128)(2,1)S(1)}, bf16[128,1024]{1,0:T(8,128)(2,1)S(1)}) custom-call(s32[8,2,8,32]{3,2,1,0:T(8,128)} %syndrome_bits.1, s32[4,16]{1,0:T(4,128)} %region_assign.1, bf16[8,32,512]{2,1,0:T(8,128)(2,1)} %state_in.1, f32[2,512]{1,0:T(2,128)} %bit_to_candidate.1, f32[2,512]{1,0:T(2,128)} %bit_to_gate.1, ...), custom_call_target="tpu_custom_call" | custom-call | tf_op jit(solution)/shard_map/window/pallas_call | solution.py:705
  63.5 0.8 %put_out.1 = (bf16[8,32,512]{2,1,0:T(8,128)(2,1)}, bf16[128,1024]{1,0:T(8,128)(2,1)}) custom-call(bf16[8,32,512]{2,1,0:T(8,128)(2,1)S(1)} %get-tuple-element.4.state_low, bf16[128,1024]{1,0:T(8,128)(2,1)S(1)} %get-tuple-element.5.context), custom_call_target="tpu_custom_call" | custom-call | tf_op jit(solution)/shard_map/put_out/pallas_call | solution.py:796
